TPU v7x, 32 devices: a whole 2x2x4 slice. The times are simulated.
32 devices in a mesh: frames: 4 (over y, core), win: 8 (over z, x).
Axes of the slice: x: 2, y: 2, z: 4, core: 2. Of those that a mesh axis runs over, the one named last changes fastest.
Arguments:
- memberships: float32 [8, 256, 4096], P('win', 'frames'), as said below
- lag_times: int32 [8], P('win'), may hold values from 1 to 8, as said below
- segment_ids: int32 [8, 256], P('win'), may hold values from 0 to 7, never falling along the last dimension, each value on 1 to 128 neighbouring positions
- bias_codes: int32 [8, 4096], P('win'), may hold values from 0 to 511
Outputs:
- free_energy: float32 [4096], P('frames')
- log_multipliers: float32 [8, 4096], P('win', 'frames')
Inputs may be any that keep to these rules, and one draw needn't show every extreme that they name: Positive; each frame's memberships sum to one up to rounding. `lag_times`: some window's lag time is 8.
All inputs are finite; a program needn't handle non-finite values.
Results may differ from a plain program's by a relative error of at most 0.00041.
Values may be sent and summed in bfloat16 or wider, within the bound.
No kernel may reach another device: no remote copies, remote signals or barrier semaphores. Data moves between devices by JAX's collectives and lax.ppermute only.
A program may use at most 64 MiB of HBM per device.

v0:
```python
import jax
import jax.numpy as jnp
from jax import lax
from jax.sharding import PartitionSpec as P

LAGMAX = 8
ITERS = 2


bias_unit = 1.0 / 128.0


def shifted(block, axis, distance):
    devices = range(lax.axis_size(axis))
    route = [(i - distance, i) for i in devices if i - distance in devices]
    return lax.ppermute(block, axis, route)


def split_rows(block, frames_dev, lag_time, valid_all):
    width = frames_dev + LAGMAX
    number = block.shape[0] // width
    states = block.shape[1]
    shaped = block.reshape(number, width, states)
    current = shaped[:, :frames_dev].reshape(number * frames_dev, states)
    later = lax.dynamic_slice_in_dim(shaped, lag_time, frames_dev, 1).reshape(
        number * frames_dev, states
    )
    later = jnp.where(valid_all[:, None], later, jnp.zeros((), later.dtype))
    return (current, later)


def add_pair(accumulated, current, later, first, rows):
    current_cols = lax.dynamic_slice_in_dim(current, first, rows, 1)
    later_cols = lax.dynamic_slice_in_dim(later, first, rows, 1)
    accumulated = jnp.einsum("tr,ts->rs", current_cols, later, preferred_element_type=jnp.float32)
    return accumulated + jnp.einsum(
        "tr,ts->rs", later_cols, current, preferred_element_type=jnp.float32
    )


def shards(memberships, lag_times, segment_ids, bias_codes):
    member = memberships[0].astype(jnp.bfloat16)
    lag_time = lag_times[0]
    segment_row = segment_ids[0]
    frames_dev = member.shape[0]
    states = member.shape[1]
    frames_all = segment_row.shape[0]
    rows = states // lax.axis_size("frames")
    position = lax.axis_index("frames")
    first = position * rows
    heading = shifted(member[:LAGMAX], "frames", -1)
    extended = jnp.concatenate([member, heading], axis=0)
    segment_ext = jnp.concatenate([segment_row, jnp.full((LAGMAX,), -1, jnp.int32)])
    valid_all = segment_row == lax.dynamic_slice_in_dim(segment_ext, lag_time, frames_all, 0)
    empty = jnp.zeros((rows, states), jnp.float32)
    current, later = split_rows(
        lax.all_gather(extended, "frames", axis=0, tiled=True), frames_dev, lag_time, valid_all
    )
    sym_counts = add_pair(empty, current, later, first, rows)
    gammas = jnp.exp(-bias_codes[0].astype(jnp.float32) * bias_unit)
    gamma_rows = lax.dynamic_slice_in_dim(gammas, first, rows, 0)
    mult_rows = jnp.sum(sym_counts, axis=1) * 0.5
    mult_full = lax.all_gather(mult_rows, "frames", axis=0, tiled=True)
    window_total = jnp.sum(mult_full)
    count_rows = lax.psum(mult_rows, "win")
    weights = jnp.full((states,), 1.0 / states, jnp.float32)
    for sweep in range(ITERS):
        scaled = gammas * weights
        scaled_rows = lax.dynamic_slice_in_dim(scaled, first, rows, 0)
        denom = mult_rows[:, None] * scaled[None, :] + scaled_rows[:, None] * mult_full[None, :]
        ratios = sym_counts / denom
        new_rows = mult_rows * jnp.sum(ratios * scaled[None, :], axis=1)
        terms = gamma_rows * jnp.sum(ratios * mult_full[None, :], axis=1)
        term_rows = lax.psum(terms, "win")
        raw_rows = count_rows / term_rows
        if sweep + 1 < ITERS:
            raw_full, mult_full = (
                lax.all_gather(raw_rows, "frames", axis=0, tiled=True),
                lax.all_gather(new_rows, "frames", axis=0, tiled=True),
            )
        else:
            raw_full = lax.all_gather(raw_rows, "frames", axis=0, tiled=True)
        weights = raw_full / jnp.sum(raw_full)
        mult_rows = new_rows
    weight_rows = lax.dynamic_slice_in_dim(weights, first, rows, 0)
    free_energy = -jnp.log(states * weight_rows)
    log_multipliers = jnp.log(mult_rows * states / window_total)[None, :]
    return (free_energy, log_multipliers)


def solution(mesh):
    placed = (P("win", "frames", None), P("win"), P("win", None), P("win", None))
    return jax.shard_map(
        shards,
        mesh=mesh,
        in_specs=placed,
        out_specs=(P("frames"), P("win", "frames")),
        check_vma=False,
    )
```

profile of v0, /device:TPU:0, one launch (start us, length us, event | category | flops | bytes accessed | tf_op | source)
XLA Modules:
  0.0 147.7 jit_solution(16507466639481832255)
XLA Ops:
  7.2 0.0 all-gather.2.cloned.1.call-start
  7.2 1.3 convert_element_type.11
  8.5 1.3 collective-permute-start
  9.8 1.3 convert_bitcast_fusion
  11.1 0.6 collective-permute-done
  11.7 0.9 pad_maximum_fusion
  12.5 0.0 all-gather.2.cloned.1.call-update
  13.2 0.8 broadcast_multiply_fusion
  14.0 0.8 fusion.6
  14.8 25.7 %all-gather.2.cloned.1.call-done = bf16[288,4096]{1,0:T(8,128)(2,1)} async-done(((bf16[72,4096]{1,0:T(8,128)(2,1)}), bf16[288,4096]{1,0:T(8,128)(2,1)}) %all-gather.2.cloned.1.call-update) | async-done | bytes 2359312 | tf_op jit(solution)/shard_map/all_gather | solution.py:57
  40.5 2.9 %fusion.10 = (bf16[4,64,4096]{2,1,0:T(8,128)(2,1)S(1)}, bf16[4,64,4096]{2,1,0:T(8,128)(2,1)S(1)}) fusion(bf16[4,72,4096]{2,1,0:T(8,128)(2,1)} %bitcast.23, s32[]{:T(128)S(6)} %select_n.20), kind=kLoop, calls=%fused_computation.30 | loop fusion | bytes 8388612 | tf_op jit(solution)/shard_map/slice | solution.py:24
  43.4 0.0 copy-start.1
  43.4 0.4 bitcast_select_fusion
  43.8 0.9 copy-done.1
  44.8 8.1 %fusion.1 = f32[1024,4096]{1,0:T(8,128)} fusion(bf16[256,4096]{1,0:T(8,128)(2,1)S(1)} %bitcast_select_fusion, bf16[256,4096]{1,0:T(8,128)(2,1)S(1)} %bitcast.21, s32[]{:T(128)S(6)} %select_n.18), kind=kOutput, calls=%fused_computation.10 | convolution fusion | flops 2147483648 | bytes 19398660 | tf_op jit(solution)/shard_map/tr,ts->rs/dot_general | solution.py:35
  52.9 7.8 %fusion.11 = (f32[1024]{0:T(1024)S(1)}, f32[1024,4096]{1,0:T(8,128)S(1)}) fusion(f32[1024,4096]{1,0:T(8,128)} %fusion.1, bf16[256,4096]{1,0:T(8,128)(2,1)} %bitcast.22, bf16[256,4096]{1,0:T(8,128)(2,1)S(1)} %bitcast_select_fusion, s32[]{:T(128)S(6)} %select_n.18), kind=kOutput, calls=%fused_computation.31 | convolution fusion | flops 2155871232 | bytes 36179972 | tf_op jit(solution)/shard_map/tr,ts->rs/dot_general | solution.py:36
  60.7 0.0 copy-start
  60.7 5.2 %all_gather.16 = f32[4096]{0:T(1024)S(1)} all-gather(f32[1024]{0:T(1024)S(1)} %broadcast_multiply_fusion.1), channel_id=1, replica_groups=mesh['frames'=4,'win'=8] {'frames'}, dimensions={0}, use_global_device_ids=true | all-gather | bytes 20480 | tf_op jit(solution)/shard_map/all_gather | solution.py:63
  65.9 0.5 copy-done
  66.4 6.2 %multiply_reduce_fusion.2 = (f32[1024]{0:T(1024)S(1)}, f32[1024]{0:T(1024)S(1)}) fusion(f32[4096]{0:T(1024)S(1)} %all_gather.16, f32[4096]{0:T(1024)S(1)} %bitcast.26, f32[1024,4096]{1,0:T(8,128)S(1)} %get-tuple-element.13, f32[1024]{0:T(1024)S(1)} %dynamic-slice_multiply_fusion, f32[1024]{0:T(1024)S(1)} %broadcast_multiply_fusion.1), kind=kLoop, calls=%fused_computation.3 | loop fusion | flops 33552384 | bytes 16826368 | tf_op jit(solution)/shard_map/reduce_sum | solution.py:73
  72.6 5.2 %all_gather.18 = f32[4096]{0:T(1024)S(1)} all-gather(f32[1024]{0:T(1024)S(1)} %fusion.9), channel_id=1, replica_groups=mesh['frames'=4,'win'=8] {'frames'}, dimensions={0}, use_global_device_ids=true | all-gather | bytes 20480 | tf_op jit(solution)/shard_map/all_gather | solution.py:79
  77.8 21.6 %all-reduce.1 = (f32[1024]{0:T(1024)S(1)}, f32[1024]{0:T(1024)S(1)}) all-reduce(f32[1024]{0:T(1024)S(1)} %broadcast_multiply_fusion.1, f32[1024]{0:T(1024)S(1)} %mul.185), channel_id=1, replica_groups=mesh['frames'=4,'win'=8] {'win'}, use_global_device_ids=true, to_apply=%region_1.2 | all-reduce | flops 2048 | bytes 16384 | tf_op jit(solution)/shard_map/psum | solution.py:65
  99.4 5.2 %all_gather.17 = f32[4096]{0:T(1024)S(1)} all-gather(f32[1024]{0:T(1024)S(1)} %div.38), channel_id=1, replica_groups=mesh['frames'=4,'win'=8] {'frames'}, dimensions={0}, use_global_device_ids=true | all-gather | bytes 20480 | tf_op jit(solution)/shard_map/all_gather | solution.py:78
  104.6 0.6 reduce_sum.79
  105.2 0.6 reduce_sum.75
  105.8 0.7 divide_multiply_fusion
  106.5 9.0 %multiply_reduce_fusion = (f32[1024]{0:T(1024)S(1)}, f32[1024]{0:T(1024)S(1)}) fusion(f32[4096]{0:T(1024)S(1)} %divide_multiply_fusion, f32[4096]{0:T(1024)S(1)} %all_gather.18, f32[1024,4096]{1,0:T(8,128)} %copy-done, f32[1024]{0:T(1024)S(1)} %dynamic_slice.33, f32[1024]{0:T(1024)S(1)} %fusion.9), kind=kLoop, calls=%fused_computation | loop fusion | flops 33552384 | bytes 16826368 | tf_op jit(solution)/shard_map/reduce_sum | solution.py:72
  115.5 17.1 %psum.23 = f32[1024]{0:T(1024)S(1)} all-reduce(f32[1024]{0:T(1024)S(1)} %mul.193), channel_id=1, replica_groups=mesh['frames'=4,'win'=8] {'win'}, use_global_device_ids=true, to_apply=%region_7.8 | all-reduce | flops 1024 | bytes 8192 | tf_op jit(solution)/shard_map/psum | solution.py:74
  132.7 5.2 %all_gather.19 = f32[4096]{0:T(1024)S(1)} all-gather(f32[1024]{0:T(1024)S(1)} %div.42), channel_id=1, replica_groups=mesh['frames'=4,'win'=8] {'frames'}, dimensions={0}, use_global_device_ids=true | all-gather | bytes 20480 | tf_op jit(solution)/shard_map/all_gather | solution.py:82
  137.9 0.6 reduce_sum.77
  138.5 1.3 fusion.5
  139.7 1.2 divide_log_fusion
  (10 shorter events, 0.1 us)
Async XLA Ops:
  7.2 33.3 %all-gather.2.cloned.1.call-start = ((), (), s32[]{:S(2)}) async-start(), calls=%async_computation | async-start | bytes 2949120 | tf_op jit(solution)/shard_map/all_gather | solution.py:57
  8.5 3.1 %collective-permute-start = (bf16[8,4096]{1,0:T(8,128)(2,1)S(1)}, bf16[8,4096]{1,0:T(8,128)(2,1)S(1)}, u32[]{:S(2)}, u32[]{:S(2)}) collective-permute-start(bf16[8,4096]{1,0:T(8,128)(2,1)S(1)} %slice_bitcast_fusion), channel_id=1, source_target_pairs={{8,0},{16,8},{24,16},{9,1},{17,9},{25,17},{10,2},{18,10},{26,18},{... | collective-permute-start | bytes 196616 | tf_op jit(solution)/shard_map/ppermute | solution.py:16
  43.4 1.4 copy-start.1
  60.7 5.7 %copy-start = (f32[1024,4096]{1,0:T(8,128)}, f32[1024,4096]{1,0:T(8,128)S(1)}, u32[]{:S(2)}) copy-start(f32[1024,4096]{1,0:T(8,128)S(1)} %get-tuple-element.13) | copy-start | bytes 50331652
Sparse Core Ops, SparseCore 0:
  12.7 27.7 all-gather.1
where the time goes:
time: 148 us
  blocking collectives  59.6 us (40%)
  waiting for transfers between devices  26.2 us (18%)
  other arithmetic  25.5 us (17%)
  matrix products  15.9 us (11%)
  between operations  14.8 us (10%)
  local copies, waits for them, and re-layouts  4.38 us (3%)
    all_gather x1, waiting for transfers between devices, shards(): lax.all_gather(extended, 'frames', axis=0, tiled=True)  25.7 us
    psum x1, blocking collectives, shards(): count_rows = lax.psum(mult_rows, 'win')  21.6 us
    psum x1, blocking collectives, shards(): term_rows = lax.psum(terms, 'win')  17.1 us
    reduce_sum x1, other arithmetic, shards(): new_rows = mult_rows * jnp.sum(ratios * scaled[None, :], axis=1)  8.98 us
    dot_general x1, matrix products, add_pair(): jnp.einsum('tr,ts->rs', current_cols, later, preferred_element_type=jnp.f...  8.12 us
    dot_general x1, matrix products, add_pair(): jnp.einsum('tr,ts->rs', later_cols, current, preferred_element_type=jnp.f...  7.76 us
    reduce_sum x1, other arithmetic, shards(): terms = gamma_rows * jnp.sum(ratios * mult_full[None, :], axis=1)  6.19 us
    all_gather x1, blocking collectives, shards(): mult_full = lax.all_gather(mult_rows, 'frames', axis=0, tiled=True)  5.21 us
  transfers between devices with their start and end apart: 2, of which 2 were waited for; matrix products, arithmetic and copies ran while one was open for 2% of the time, Pallas kernels for 0%

commit v1 on v0

v1 whole, which is shorter than its diff:
```python
import jax
import jax.numpy as jnp
from jax import lax
from jax.experimental import pallas as pl
from jax.experimental.pallas import tpu as pltpu
from jax.sharding import PartitionSpec as P

ITERS = 2
LANES = 128

bias_unit = 1.0 / 128.0


def split3(x):
    high = x.astype(jnp.bfloat16)
    rest = x - high.astype(jnp.float32)
    middle = rest.astype(jnp.bfloat16)
    low = (rest - middle.astype(jnp.float32)).astype(jnp.bfloat16)
    return jnp.concatenate([high, middle, low], axis=0)


def exact_dot(x, matrix):
    out = jnp.dot(split3(x), matrix, preferred_element_type=jnp.float32)
    number = x.shape[0]
    return (out[:number] + out[number : 2 * number]) + out[2 * number :]


def column_of(row):
    rows = row.shape[1]
    return jnp.transpose(jnp.broadcast_to(row, (LANES, rows)))


def row_of(partial):
    return jnp.sum(jnp.transpose(partial), axis=0, keepdims=True)


def column_tile(states):
    for width in (512, 256, 128):
        if states % width == 0:
            return width
    return states


def add_tile(counts, ratio_col, ratio_row, plain_ref, scaled_ref):
    rows, width = counts.shape
    plain = plain_ref[...]
    scaled = scaled_ref[...]
    for lane in range(0, width, LANES):
        r_row = ratio_row[:, lane : lane + LANES]
        part = counts[:, lane : lane + LANES] / (ratio_col + r_row)
        plain = plain + part
        scaled = scaled + part * r_row
    plain_ref[...] = plain
    scaled_ref[...] = scaled


def first_kernel(where, moved, joined, codes, *refs):
    blocks = refs[:-11]
    counts_out, mult_out, terms_out, ratio_out = refs[-11:-7]
    pair, left, ratio_row, ratio_col, plain, scaled, sem = refs[-7:]
    frames_all, states = moved.shape[0], pair.shape[1]
    rows = left.shape[0]
    frames_dev = blocks[0].shape[0]
    copies = [
        pltpu.make_async_copy(
            block, pair.at[pl.ds(frames_all + i * frames_dev, frames_dev), :], sem.at[i]
        )
        for i, block in enumerate(blocks)
    ]
    for copy in copies:
        copy.start()
    for copy in copies:
        copy.wait()
    first = pl.multiple_of(where[0] * rows, LANES)
    member = pair[pl.ds(frames_all, frames_all), :]
    ones = jnp.ones((8, states), jnp.bfloat16)
    sums = lax.dot_general(ones, member, (((1,), (1,)), ((), ())), preferred_element_type=jnp.float32)
    near = exact_dot(sums, joined[...])
    mult = exact_dot(near, member)[:1] * 0.5
    gammas = jnp.exp(codes[...].astype(jnp.float32) * -bias_unit)
    mult_out[...] = mult
    ratio_row[...] = gammas * (1.0 / states) / mult
    pair[pl.ds(0, frames_all), :] = jnp.dot(
        moved[...], member, preferred_element_type=jnp.float32
    ).astype(jnp.bfloat16)
    own = pl.ds(first, rows)
    left[:, :frames_all] = jnp.transpose(pair[pl.ds(frames_all, frames_all), own])
    left[:, frames_all:] = jnp.transpose(pair[pl.ds(0, frames_all), own])
    ratio_col[...] = column_of(ratio_row[:, own])
    plain[...] = jnp.zeros_like(plain)
    scaled[...] = jnp.zeros_like(scaled)
    width = column_tile(states)

    @pl.loop(0, states // width)
    def _(step):
        columns = pl.ds(pl.multiple_of(step * width, width), width)
        tile = jnp.dot(left[...], pair[:, columns], preferred_element_type=jnp.float32)
        counts_out[:, columns] = tile
        add_tile(tile, ratio_col[...], ratio_row[:, columns], plain, scaled)

    gamma_own = jnp.exp(codes[:, own].astype(jnp.float32) * -bias_unit)
    terms = gamma_own / mult_out[:, own] * row_of(plain[...])
    terms_out[...] = terms
    ratio_out[...] = row_of(scaled[...]) * states / terms


def second_kernel(where, given, mult, codes, counts, terms_out, logs_out, state_counts, new_mult, ratio_row, ratio_col, plain, scaled):
    rows = terms_out.shape[1]
    states = codes.shape[1]
    number = given.shape[0] // (states // rows)
    own_window = lax.broadcasted_iota(jnp.int32, (number, rows), 0) == where[1]
    gammas = jnp.exp(codes[...].astype(jnp.float32) * -bias_unit)
    for block in range(states // rows):
        here = slice(block * rows, (block + 1) * rows)
        mults = given[block * number : (block + 1) * number, :rows]
        others = given[block * number : (block + 1) * number, rows:]
        part = 2.0 * mults / (1.0 + others)
        terms = jnp.where(own_window, part * states, others)
        new_mult[:, here] = jnp.sum(jnp.where(own_window, part * others, 0.0), axis=0, keepdims=True)
        total = jnp.sum(mults, axis=0, keepdims=True)
        state_counts[:, here] = total
        ratio_row[:, here] = total / jnp.sum(terms, axis=0, keepdims=True)
    raw = ratio_row[...]
    weights = raw / jnp.sum(raw)
    ratio_row[...] = gammas * weights / new_mult[...]
    own = pl.ds(pl.multiple_of(where[0] * rows, LANES), rows)
    ratio_col[...] = column_of(ratio_row[:, own])
    plain[...] = jnp.zeros_like(plain)
    scaled[...] = jnp.zeros_like(scaled)
    width = column_tile(states)

    @pl.loop(0, states // width)
    def _(step):
        columns = pl.ds(pl.multiple_of(step * width, width), width)
        add_tile(counts[:, columns], ratio_col[...], ratio_row[:, columns], plain, scaled)

    gamma_own = jnp.exp(codes[:, own].astype(jnp.float32) * -bias_unit)
    terms_out[...] = gamma_own / new_mult[:, own] * row_of(plain[...])
    window_total = jnp.sum(mult[...])
    logs_out[...] = jnp.log(row_of(scaled[...]) * states / window_total)


def last_kernel(where, given, state_counts, energy_out, raw_row):
    rows = energy_out.shape[1]
    states = state_counts.shape[1]
    number = given.shape[0] // (states // rows)
    for block in range(states // rows):
        here = slice(block * rows, (block + 1) * rows)
        terms = jnp.sum(given[block * number : (block + 1) * number, :], axis=0, keepdims=True)
        raw_row[:, here] = state_counts[:, here] / terms
    own = pl.ds(pl.multiple_of(where[0] * rows, LANES), rows)
    total = jnp.sum(raw_row[...])
    energy_out[...] = -jnp.log(raw_row[:, own] / total * states)


def vector(width, dtype=jnp.float32):
    return jax.ShapeDtypeStruct((1, width), dtype)


def scratch(*shape, dtype=jnp.float32):
    return pltpu.VMEM(shape, dtype)


def everyone(block):
    return lax.all_to_all(block, ("frames", "win"), 0, 0, tiled=True)


def shards(memberships, lag_times, segment_ids, bias_codes):
    member = memberships[0].astype(jnp.bfloat16)
    frames_dev, states = member.shape
    frames_all = segment_ids.shape[1]
    number = lax.axis_size("frames")
    windows = lax.axis_size("win")
    rows = states // number
    position = lax.axis_index("frames")
    window = lax.axis_index("win")
    lag_time = lag_times[0]
    partner = [(i, i ^ 1) for i in range(number)]
    blocks = []
    order = []
    for step in range(0, number, 2):
        if step == 0:
            near = member
        else:
            near = lax.ppermute(member, "frames", [((i + step) % number, i) for i in range(number)])
        blocks.append(near)
        order.append((position + step) % number)
    for step in range(number // 2):
        blocks.insert(2 * step + 1, lax.ppermute(blocks[2 * step], "frames", partner))
        order.insert(2 * step + 1, order[2 * step] ^ 1)
    places = jnp.concatenate([block * frames_dev + jnp.arange(frames_dev) for block in order])
    segments = jnp.concatenate(
        [lax.dynamic_slice_in_dim(segment_ids[0], block * frames_dev, frames_dev, 0) for block in order]
    )
    same = segments[:, None] == segments[None, :]
    ahead = same & (places[None, :] == places[:, None] + lag_time)
    behind = same & (places[None, :] + lag_time == places[:, None])
    moved = ahead.astype(jnp.bfloat16)
    joined = (ahead | behind).astype(jnp.bfloat16)
    where = jnp.stack([position, window]).astype(jnp.int32)
    smem = pl.BlockSpec(memory_space=pltpu.SMEM)
    vmem = pl.BlockSpec(memory_space=pltpu.VMEM)
    hbm = pl.BlockSpec(memory_space=pl.ANY)
    sums = [scratch(1, states), scratch(rows, LANES), scratch(rows, LANES), scratch(rows, LANES)]
    counts, mult, terms, odds = pl.pallas_call(
        first_kernel,
        out_shape=(
            COUNTS((rows, states), jnp.float32),
            vector(states),
            vector(rows),
            vector(rows),
        ),
        in_specs=[smem, vmem, vmem, vmem] + [hbm] * number,
        out_specs=(vmem,) * 4,
        scratch_shapes=[
            scratch(2 * frames_all, states, dtype=jnp.bfloat16),
            scratch(rows, 2 * frames_all, dtype=jnp.bfloat16),
        ]
        + sums
        + [pltpu.SemaphoreType.DMA((number,))],
        compiler_params=pltpu.CompilerParams(vmem_limit_bytes=40 << 20),
        name="first",
    )(where, moved, joined, bias_codes, *blocks)
    mult_rows = lax.dynamic_slice_in_dim(mult, position * rows, rows, 1)
    target = lax.broadcasted_iota(jnp.int32, (number * windows, 1), 0) % windows
    sent = jnp.where(target == window, odds, terms)
    sent = jnp.concatenate([jnp.broadcast_to(mult_rows, sent.shape), sent], axis=1)
    given = everyone(sent)
    terms, logs, state_counts = pl.pallas_call(
        second_kernel,
        out_shape=(vector(rows), vector(rows), vector(states)),
        in_specs=[smem, vmem, vmem, vmem, vmem],
        out_specs=(vmem,) * 3,
        scratch_shapes=[scratch(1, states)] + sums,
        compiler_params=pltpu.CompilerParams(vmem_limit_bytes=40 << 20),
        name="second",
    )(where, given, mult, bias_codes, counts)
    given = everyone(jnp.broadcast_to(terms, (number * windows, rows)))
    energy = pl.pallas_call(
        last_kernel,
        out_shape=vector(rows),
        in_specs=[smem, vmem, vmem],
        out_specs=vmem,
        scratch_shapes=[scratch(1, states)],
        name="last",
    )(where, given, state_counts)
    return energy[0], logs


COUNTS = jax.ShapeDtypeStruct


def solution(mesh):
    placed = (P("win", "frames", None), P("win"), P("win", None), P("win", None))
    return jax.shard_map(
        shards,
        mesh=mesh,
        in_specs=placed,
        out_specs=(P("frames"), P("win", "frames")),
        check_vma=False,
    )
```

time: 148 us -> 77.7 us (0.53)
  blocking collectives: 59.6 us -> 26.5 us
  Pallas kernels: 0 us -> 28.8 us
  other arithmetic: 25.5 us -> 1.73 us
  matrix products: 15.9 us -> 0 us
  waiting for transfers between devices: 26.2 us -> 11.9 us
  between operations: 14.8 us -> 1.42 us
  starting transfers between devices: 1.33 us -> 3.07 us
    psum x2 -> x0, blocking collectives: 38.7 us -> none  [the longest x1 21.6 us: shards(): count_rows = lax.psum(mult_rows, 'win')]
    pallas_call x0 -> x3, Pallas kernels: none -> 28.8 us  [the longest x1 16.5 us: shards(): pl.pallas_call(first_kernel, out_shape=(COUNTS((rows, states), jnp.float3...]
    all_to_all x0 -> x2, blocking collectives: none -> 26.5 us  [everyone(): return lax.all_to_all(block, ('frames', 'win'), 0, 0, tiled=True)]
    all_gather x1 -> x0, waiting for transfers between devices: 25.7 us -> none  [shards(): lax.all_gather(extended, 'frames', axis=0, tiled=True)]
    all_gather x4 -> x0, blocking collectives: 20.8 us -> none  [the longest x1 5.21 us: shards(): mult_full = lax.all_gather(mult_rows, 'frames', axis=0, tiled=True)]
    reduce_sum x5 -> x0, other arithmetic: 17 us -> none  [the longest x1 8.98 us: shards(): new_rows = mult_rows * jnp.sum(ratios * scaled[None, :], axis=1)]
    dot_general x2 -> x0, matrix products: 15.9 us -> none  [the longest x1 8.12 us: add_pair(): jnp.einsum('tr,ts->rs', current_cols, later, preferred_element_type=jnp.f...]
    ppermute x1 -> x3, waiting for transfers between devices: 0.56 us -> 11.9 us  [the longest x1 11.2 us: shards(): lax.ppermute(member, 'frames', [((i + step) % number, i) for i in range(n...]
  transfers between devices with their start and end apart: 2 -> 3, of which waited for: 2 -> 2; matrix products, arithmetic and copies ran while one was open for 2% -> 1% of each run, Pallas kernels for 0% -> 0%
where the time goes in v1:
time: 77.7 us; the launch traced here: 77.3 us
  Pallas kernels  28.8 us (37%)
  blocking collectives  26.5 us (34%)
  waiting for transfers between devices  11.9 us (15%)
  local copies, waits for them, and re-layouts  3.85 us (5%)
  starting transfers between devices  3.07 us (4%)
  other arithmetic  1.73 us (2%)
  between operations  1.42 us (2%)
    all_to_all x2, blocking collectives, everyone(): return lax.all_to_all(block, ('frames', 'win'), 0, 0, tiled=True)  26.5 us
    pallas_call x1, Pallas kernels, shards(): pl.pallas_call(first_kernel, out_shape=(COUNTS((rows, states), jnp.float3...  16.5 us
    ppermute x1, waiting for transfers between devices, shards(): lax.ppermute(member, 'frames', [((i + step) % number, i) for i in range(n...  11.2 us
    pallas_call x1, Pallas kernels, shards(): pl.pallas_call(second_kernel, out_shape=(vector(rows), vector(rows), vect...  10.6 us
    ppermute x1, starting transfers between devices, shards(): lax.ppermute(member, 'frames', [((i + step) % number, i) for i in range(n...  3.06 us
    unnamed x10, local copies, waits for them, and re-layouts  2.78 us
    pallas_call x1, Pallas kernels, shards(): pl.pallas_call(last_kernel, out_shape=vector(rows), in_specs=[smem, vmem,...  1.71 us
  transfers between devices with their start and end apart: 3, of which 2 were waited for; matrix products, arithmetic and copies ran while one was open for 1% of the time, Pallas kernels for 0%

profile of v1, /device:TPU:0, one launch (start us, length us, event | category | flops | bytes accessed | tf_op | source)
XLA Modules:
  0.0 77.3 jit_solution(14604802775747411373)
XLA Ops:
  0.6 1.3 %convert_bitcast_fusion.refs_0_ = bf16[64,4096]{1,0:T(8,128)(2,1)S(1)} fusion(f32[1,64,4096]{2,1,0:T(8,128)} %param.4), kind=kLoop, calls=%fused_computation | loop fusion | flops 262144 | bytes 1572864 | tf_op jit(solution)/shard_map/convert_element_type | solution.py:169
  1.9 3.1 %collective-permute-start.1 = (bf16[64,4096]{1,0:T(8,128)(2,1)S(1)}, bf16[64,4096]{1,0:T(8,128)(2,1)S(1)}, u32[]{:S(2)}, u32[]{:S(2)}) collective-permute-start(bf16[64,4096]{1,0:T(8,128)(2,1)S(1)} %convert_bitcast_fusion.refs_0_), channel_id=1, source_target_pairs={{16,0},{24,8},{0,16},{8,24},{17,1},{25,9},{1,17},{9,25},{18,2},{26... | collective-permute-start | bytes 1572872 | tf_op jit(solution)/shard_map/ppermute | solution.py:185
  5.0 0.0 collective-permute-start
  5.7 11.2 %collective-permute-done.1.refs_2_ = bf16[64,4096]{1,0:T(8,128)(2,1)S(1)} collective-permute-done((bf16[64,4096]{1,0:T(8,128)(2,1)S(1)}, bf16[64,4096]{1,0:T(8,128)(2,1)S(1)}, u32[]{:S(2)}, u32[]{:S(2)}) %collective-permute-start.1) | collective-permute-done | bytes 524320 | tf_op jit(solution)/shard_map/ppermute | solution.py:185
  16.9 0.0 collective-permute-start.2
  16.9 0.1 pad_add_fusion.2.where
  17.0 0.0 copy-start.3
  17.0 0.8 %fusion.3 = (s32[64]{0:T(128)S(1)}, s32[64]{0:T(128)S(1)}, s32[64]{0:T(128)S(1)}, s32[64]{0:T(128)S(1)}) fusion(s32[1,256]{1,0:T(1,128)} %param.6, s32[]{:T(128)S(6)} %select_n.42, s32[]{:T(128)S(6)} %select_n.43, s32[]{:T(128)S(6)} %select_n.46, s32[]{:T(128)S(6)} %select_n.45), kind=kLoop, calls=%fused_computation.18 | loop fusion | bytes 2064 | tf_op jit(solution)/shard_map/dynamic_slice | solution.py:193
  17.8 0.1 broadcast_add_fusion
  17.9 0.2 fusion.1
  18.0 0.0 collective-permute-done.refs_1_
  18.1 0.7 collective-permute-done.2.refs_3_
  18.8 0.0 copy-start
  18.8 0.7 copy-done
  19.5 16.5 %first.1 = (f32[1024,4096]{1,0:T(8,128)}, f32[1,4096]{1,0:T(1,128)S(1)}, f32[1,1024]{1,0:T(1,128)S(1)}, f32[1,1024]{1,0:T(1,128)S(1)}) custom-call(s32[2]{0:T(128)S(1)} %pad_add_fusion.2.where, bf16[256,256]{1,0:T(8,128)(2,1)S(1)} %get-tuple-element.19.moved, bf16[256,256]{1,0:T(8,128)(2,1)S(1)} %get-tuple-element.18.joined, s32[1,4096]{1,0:T(1,128)S(1)} %copy-done, ...), custom_call_target="tpu_custom_call" | custom-call | tf_op jit(solution)/shard_map/first/pallas_call | solution.py:205
  36.1 0.1 broadcast_select_fusion
  36.2 0.2 all_to_all.12
  36.4 16.3 %all_to_all.19 = f32[32,1,2048]{2,1,0:T(1,128)S(1)} all-to-all(f32[32,1,2048]{2,1,0:T(1,128)S(1)} %all_to_all.12), channel_id=1, replica_groups=mesh['frames'=4,'win'=8] {'frames','win'}, dimensions={0} | all-to-all | bytes 524288 | tf_op jit(solution)/shard_map/all_to_all | solution.py:165
  52.7 0.1 copy.10
  52.8 0.0 copy-start.1
  52.8 0.7 copy-done.1
  53.5 10.6 %second.1 = (f32[1,1024]{1,0:T(1,128)S(1)}, f32[1,1024]{1,0:T(1,128)}, f32[1,4096]{1,0:T(1,128)S(1)}) custom-call(s32[2]{0:T(128)S(1)} %pad_add_fusion.2.where, f32[32,2048]{1,0:T(8,128)S(1)} %bitcast.25, f32[1,4096]{1,0:T(1,128)S(1)} %get-tuple-element.9.mult, s32[1,4096]{1,0:T(1,128)S(1)} %copy-done.1, f32[1024,4096]{1,0:T(8,128)} %get-tuple-element.12.counts), custom_call_target="tpu_custom_call" | custom-call | tf_op jit(solution)/shard_map/second/pallas_call | solution.py:229
  64.1 0.0 copy-start.2
  64.1 0.6 copy-done.2
  64.7 0.1 broadcast_in_dim.53
  64.8 10.1 %all_to_all.20 = f32[32,1,1024]{2,1,0:T(1,128)S(1)} all-to-all(f32[32,1,1024]{2,1,0:T(1,128)S(1)} %broadcast_in_dim.53), channel_id=1, replica_groups=mesh['frames'=4,'win'=8] {'frames','win'}, dimensions={0} | all-to-all | bytes 262144 | tf_op jit(solution)/shard_map/all_to_all | solution.py:165
  74.9 0.7 copy.11
  75.6 0.0 copy-done.3
  75.6 1.7 %last.1 = f32[1,1024]{1,0:T(1,128)} custom-call(s32[2]{0:T(128)} %copy-done.3, f32[32,1024]{1,0:T(8,128)} %bitcast.29, f32[1,4096]{1,0:T(1,128)} %copy-done.2), custom_call_target="tpu_custom_call" | custom-call | tf_op jit(solution)/shard_map/last/pallas_call | solution.py:239
  (8 shorter events, 0.1 us)
Async XLA Ops:
  1.9 15.0 %collective-permute-start.1 = (bf16[64,4096]{1,0:T(8,128)(2,1)S(1)}, bf16[64,4096]{1,0:T(8,128)(2,1)S(1)}, u32[]{:S(2)}, u32[]{:S(2)}) collective-permute-start(bf16[64,4096]{1,0:T(8,128)(2,1)S(1)} %convert_bitcast_fusion.refs_0_), channel_id=1, source_target_pairs={{16,0},{24,8},{0,16},{8,24},{17,1},{25,9},{1,17},{9,25},{18,2},{26... | collective-permute-start | bytes 1572872 | tf_op jit(solution)/shard_map/ppermute | solution.py:185
  5.0 13.1 %collective-permute-start = (bf16[64,4096]{1,0:T(8,128)(2,1)S(1)}, bf16[64,4096]{1,0:T(8,128)(2,1)S(1)}, u32[]{:S(2)}, u32[]{:S(2)}) collective-permute-start(bf16[64,4096]{1,0:T(8,128)(2,1)S(1)} %convert_bitcast_fusion.refs_0_), channel_id=1, source_target_pairs={{0,8},{8,0},{16,24},{24,16},{1,9},{9,1},{17,25},{25,17},{2,10},{10... | collective-permute-start | bytes 1572872 | tf_op jit(solution)/shard_map/ppermute | solution.py:189
  16.9 1.9 %collective-permute-start.2 = (bf16[64,4096]{1,0:T(8,128)(2,1)S(1)}, bf16[64,4096]{1,0:T(8,128)(2,1)S(1)}, u32[]{:S(2)}, u32[]{:S(2)}) collective-permute-start(bf16[64,4096]{1,0:T(8,128)(2,1)S(1)} %collective-permute-done.1.refs_2_), channel_id=1, source_target_pairs={{0,8},{8,0},{16,24},{24,16},{1,9},{9,1},{17,25},{25,17},{2,10},{10... | collective-permute-start | bytes 1572872 | tf_op jit(solution)/shard_map/ppermute | solution.py:189
  17.0 58.6 %copy-start.3 = (s32[2]{0:T(128)}, s32[2]{0:T(128)S(1)}, u32[]{:S(2)}) copy-start(s32[2]{0:T(128)S(1)} %pad_add_fusion.2.where) | copy-start | bytes 28
  18.8 0.7 copy-start
  52.8 0.7 copy-start.1
  64.1 0.6 copy-start.2

commit v2 on v0

v2 whole, which is shorter than its diff:
```python
import math

import jax
import jax.numpy as jnp
from jax import lax
from jax.experimental import pallas as pl
from jax.experimental.pallas import tpu as pltpu
from jax.sharding import PartitionSpec as P


LANES = 128
PIECES = 4

bias_unit = 1.0 / 128.0


def chunk_bounds(states, group):
    return [(0, group), (group, states)] if states > group else [(0, states)]


def granule(states, group):
    size = group
    for low, high in chunk_bounds(states, group):
        size = math.gcd(size, high - low)
    return size


def wrapped(place, states):
    return jnp.where(place >= states, place - states, place)


def split3(x):
    high = x.astype(jnp.bfloat16)
    rest = x - high.astype(jnp.float32)
    middle = rest.astype(jnp.bfloat16)
    low = (rest - middle.astype(jnp.float32)).astype(jnp.bfloat16)
    return high, middle, low


def gamma_of(codes):
    return jnp.exp(codes.astype(jnp.float32) * -bias_unit)


def spread(folded, column_ref):
    for i in range(folded.shape[0]):
        square = jnp.broadcast_to(folded[i : i + 1, :], (LANES, LANES))
        column_ref[i * LANES : (i + 1) * LANES, :] = jnp.transpose(square)


def gathered(partial_ref):
    rows = partial_ref.shape[0]
    return jnp.concatenate(
        [
            jnp.sum(jnp.transpose(partial_ref[i : i + LANES, :]), axis=0, keepdims=True)
            for i in range(0, rows, LANES)
        ],
        axis=0,
    )


def column_tile(width):
    for tile in (512, 256, 128):
        if width % tile == 0:
            return tile


def add_tile(counts, ratio_col, ratio_rows, plain_ref, scaled_ref):
    plain = plain_ref[...]
    scaled = scaled_ref[...]
    for i, r_row in enumerate(ratio_rows):
        part = counts[:, i * LANES : (i + 1) * LANES] / (ratio_col + r_row)
        plain = plain + part
        scaled = scaled + part * r_row
    plain_ref[...] = plain
    scaled_ref[...] = scaled


def place():
    position = lax.axis_index("frames")
    return position, lax.axis_index("win"), position % 2, position // 2


def fetched(sources, targets, sem):
    copies = [pltpu.make_async_copy(a, b, sem.at[i]) for i, (a, b) in enumerate(zip(sources, targets))]
    for copy in copies:
        copy.start()
    for copy in copies:
        copy.wait()


def prepare_kernel(group, given, *outs):
    member, sem = outs[-2:]
    whole, parts = outs[0], outs[1:-2]
    height = given.shape[1] // PIECES
    pieces = [pl.ds(i * height, height) for i in range(PIECES)]
    fetched([given.at[:, piece, :] for piece in pieces], [member.at[:, piece, :] for piece in pieces], sem)
    frames_dev, states = member.shape[1:]
    bounds = chunk_bounds(states, group)
    size = granule(states, group)
    own_chip = place()[3]
    total = jnp.zeros((frames_dev, LANES), jnp.float32)
    for j in range(0, states, size):
        source = pl.multiple_of(wrapped(own_chip * group + j, states), size)
        block = member[0, :, pl.ds(source, size)].astype(jnp.bfloat16)
        whole[:, j : j + size] = block
        wide = block.astype(jnp.float32)
        for i in range(0, size, LANES):
            total = total + wide[:, i : i + LANES]
    sums = jnp.broadcast_to(jnp.sum(total, axis=1, keepdims=True), (frames_dev, LANES))
    high, middle, low = split3(sums)
    lane = lax.broadcasted_iota(jnp.int32, sums.shape, 1)
    none = jnp.zeros_like(sums)
    packed = jnp.where(lane == 0, high.astype(jnp.float32), none)
    packed = jnp.where(lane == 1, middle.astype(jnp.float32), packed)
    packed = jnp.where(lane == 2, low.astype(jnp.float32), packed).astype(jnp.bfloat16)
    whole[:, states:] = packed
    for chip in range(1, states // group):
        base = (own_chip - chip) * group
        base = jnp.where(base < 0, base + states, base)
        for c, (low_end, high_end) in enumerate(bounds):
            part = parts[(chip - 1) * len(bounds) + c]
            for j in range(low_end, high_end, size):
                source = pl.multiple_of(wrapped(base + j, states), size)
                part[:, j - low_end : j - low_end + size] = member[0, :, pl.ds(source, size)].astype(jnp.bfloat16)
            if c == 0:
                part[:, high_end:] = packed


def plan_kernel(number, group, lag, segments_in, codes_in, inner, outer, joined, gammas, segments, codes, sem):
    fetched([segments_in, codes_in], [segments, codes], sem)
    frames_all = segments.shape[1]
    frames_dev = frames_all // number
    near = 2 * frames_dev
    _, _, core, own_chip = place()
    lag_time = lag[0]
    grid = (frames_all, frames_all)
    row = lax.broadcasted_iota(jnp.int32, grid, 0)
    frame = row
    for i in range(number):
        owner = lax.rem(own_chip + i // 2, number // 2) * 2 + (core if i % 2 == 0 else 1 - core)
        inside = (row >= i * frames_dev) & (row < (i + 1) * frames_dev)
        frame = jnp.where(inside, row + (owner - i) * frames_dev, frame)
    frame = frame.astype(jnp.float32)
    seg_row = jnp.broadcast_to(segments[...].astype(jnp.float32), grid)
    col = lax.broadcasted_iota(jnp.int32, grid, 1).astype(jnp.float32)
    seg = jnp.sum(jnp.where(frame == col, seg_row, 0.0), axis=1, keepdims=True)
    seg_from = jnp.broadcast_to(seg, grid)
    seg_to = jnp.transpose(seg_from)
    frame_to = jnp.transpose(frame)
    ahead = frame_to - frame
    same = seg_from == seg_to
    lag_float = lag_time.astype(jnp.float32)
    forward = same & (ahead == lag_float)
    backward = same & (ahead == -lag_float)
    joined[...] = jnp.where(forward | backward, 1.0, 0.0).astype(jnp.bfloat16)
    forward = jnp.where(forward, 1.0, 0.0)
    inner[...] = forward[:near, :near].astype(jnp.bfloat16)
    if number > 2:
        below = frame < (own_chip * near).astype(jnp.float32)
        touching = jnp.where(below, forward, jnp.where(backward, 1.0, 0.0))
        outer[...] = touching[near:, :].astype(jnp.bfloat16)
    size = granule(codes.shape[0] * LANES, group) // LANES
    for i in range(0, codes.shape[0], size):
        start = wrapped(own_chip * (group // LANES) + i, codes.shape[0])
        gammas[i : i + size, :] = gamma_of(codes[pl.ds(pl.multiple_of(start, size), size), :])


def near_kernel(bounds, whole, beside, inner, *refs):
    counts = refs[: len(bounds)]
    pair, left = refs[len(bounds) :]
    frames_dev = whole.shape[0]
    near = 2 * frames_dev
    rows = left.shape[0]
    states = pair.shape[1]
    own = pl.ds(pl.multiple_of(place()[2] * rows, rows), rows)
    pair[near : near + frames_dev, :] = whole[:, :states]
    pair[near + frames_dev :, :] = beside[:, :states]
    pair[:near, :] = jnp.dot(inner[...], pair[near:, :], preferred_element_type=jnp.float32).astype(jnp.bfloat16)
    left[:, :near] = jnp.transpose(pair[near:, own])
    left[:, near:] = jnp.transpose(pair[:near, own])
    for (low_end, high_end), count in zip(bounds, counts):
        tile = column_tile(high_end - low_end)

        @pl.loop(0, (high_end - low_end) // tile)
        def _(step):
            here = pl.ds(pl.multiple_of(step * tile, tile), tile)
            there = pl.ds(pl.multiple_of(low_end + step * tile, tile), tile)
            count[:, here] = jnp.dot(left[...], pair[:, there], preferred_element_type=jnp.float32)


def counts_kernel(bounds, which, number, *refs):
    low_end, high_end = bounds[which]
    width = high_end - low_end
    is_first, is_last = which == 0, which == len(bounds) - 1
    refs = list(refs)
    take = lambda k: [refs.pop(0) for _ in range(k)]
    gammas, counts_in = take(2)
    blocks = take(number)
    far = number > 2
    if is_first:
        outer, joined = take(2) if far else take(1) * 2
    else:
        plain_in, scaled_in, column, left, outer, mult_own_ref = take(6)
    counts_out, mult_out = take(2)
    if not is_last:
        plain, scaled = take(2)
    if is_first and not is_last:
        column, left, steps = take(3)
        mult_own_ref = mult_out
    if is_last:
        (sent,) = take(1)
        plain, scaled = take(2)
    if is_first and is_last:
        column, left, steps = take(3)
        mult_own_ref = mult_out
    pair, ratio = take(2)
    frames_dev = blocks[0].shape[0]
    frames_all = number * frames_dev
    away = frames_all - 2 * frames_dev
    rows = plain.shape[0]
    states = gammas.shape[0] * LANES
    depth = rows // LANES
    _, window, core, _ = place()
    own_rows = pl.ds(pl.multiple_of(core * depth, depth), depth)
    tile = column_tile(width)
    if is_first:
        sums = [block[:, states:] for block in blocks[:2]] + [block[:, width:] for block in blocks[2:]]
        column_sums = jnp.dot(joined[...], jnp.concatenate(sums, axis=0), preferred_element_type=jnp.float32)
        turned = jnp.transpose(column_sums)
        line = turned[0:1] + turned[1:2] + turned[2:3]
        parts = [jnp.broadcast_to(part.astype(jnp.float32), (16, frames_all)).astype(jnp.bfloat16) for part in split3(line)]
        steps[:48, :] = jnp.concatenate(parts, axis=0)
        if away:
            steps[48:, :] = outer[...]
        step_matrix = steps
    else:
        step_matrix = outer
    for j in range(0, width, tile):
        local = [block[:, low_end + j : low_end + j + tile] for block in blocks[:2]]
        others = [block[:, j : j + tile] for block in blocks[2:]]
        member = jnp.concatenate(local + others, axis=0)
        product = jnp.dot(step_matrix[...], member, preferred_element_type=jnp.float32)
        mult_row = (product[0:1] + product[16:17] + product[32:33]) * 0.5
        for i in range(tile // LANES):
            mult_out[j // LANES + i : j // LANES + i + 1, :] = mult_row[:, i * LANES : (i + 1) * LANES]
        if away:
            pair[:away, j : j + tile] = product[48:].astype(jnp.bfloat16)
            pair[away:, j : j + tile] = jnp.concatenate(others, axis=0)
    ratio[...] = gammas[low_end // LANES : high_end // LANES, :] * (1.0 / states) / mult_out[...]
    if is_first:
        own = pl.ds(pl.multiple_of(core * rows, rows), rows)
        if away:
            left[:, :away] = jnp.transpose(pair[away:, own])
            left[:, away:] = jnp.transpose(pair[:away, own])
        spread(ratio[own_rows, :], column)
        plain[...] = jnp.zeros_like(plain)
        scaled[...] = jnp.zeros_like(scaled)
    else:
        plain[...] = plain_in[...]
        scaled[...] = scaled_in[...]

    @pl.loop(0, width // tile)
    def _(step):
        columns = pl.ds(pl.multiple_of(step * tile, tile), tile)
        counts = counts_in[:, columns]
        if away:
            counts = counts + jnp.dot(left[...], pair[:, columns], preferred_element_type=jnp.float32)
        counts_out[:, columns] = counts
        ratio_rows = [ratio[pl.ds(step * (tile // LANES) + i, 1), :] for i in range(tile // LANES)]
        add_tile(counts, column[...], ratio_rows, plain, scaled)

    if is_last:
        mult_own = mult_own_ref[own_rows, :]
        terms = gammas[own_rows, :] / mult_own * gathered(plain)
        odds = gathered(scaled) * states / terms
        windows = sent.shape[0] // number

        @pl.loop(0, sent.shape[0])
        def _(target):
            sent[target, :depth] = mult_own
            sent[target, depth:] = jnp.where(lax.rem(target, windows) == window, odds, terms)


def second_kernel(bounds, *refs):
    number_chunks = len(bounds)
    given, gammas = refs[:2]
    mults = refs[2 : 2 + number_chunks]
    counts = refs[2 + number_chunks : 2 + 2 * number_chunks]
    sent, logs_out, state_counts, new_mult, ratio, column, plain, scaled = refs[2 + 2 * number_chunks :]
    depth = logs_out.shape[0]
    states = gammas.shape[0] * LANES
    number = gammas.shape[0] // depth
    windows = given.shape[0] // number
    _, window, core, own_chip = place()
    own_window = lax.broadcasted_iota(jnp.int32, (windows, depth, LANES), 0) == window
    for block in range(number):
        here = pl.ds(pl.multiple_of(lax.rem(block + (number - 2 * own_chip), number) * depth, depth), depth)
        block_mult = given[block * windows : (block + 1) * windows, :depth]
        others = given[block * windows : (block + 1) * windows, depth:]
        part = 2.0 * block_mult / (1.0 + others)
        terms = jnp.where(own_window, part * states, others)
        new_mult[here, :] = jnp.sum(jnp.where(own_window, part * others, 0.0), axis=0)
        total = jnp.sum(block_mult, axis=0)
        state_counts[block * depth : (block + 1) * depth, :] = total
        ratio[here, :] = total / jnp.sum(terms, axis=0)
    raw = ratio[...]
    weights = raw / jnp.sum(raw)
    ratio[...] = gammas[...] * weights / new_mult[...]
    own = pl.ds(pl.multiple_of(core * depth, depth), depth)
    spread(ratio[own, :], column)
    plain[...] = jnp.zeros_like(plain)
    scaled[...] = jnp.zeros_like(scaled)
    for (low_end, high_end), count in zip(bounds, counts):
        width = high_end - low_end
        tile = column_tile(width)

        @pl.loop(0, width // tile)
        def _(step):
            columns = pl.ds(pl.multiple_of(step * tile, tile), tile)
            start = low_end // LANES + step * (tile // LANES)
            ratio_rows = [ratio[pl.ds(start + i, 1), :] for i in range(tile // LANES)]
            add_tile(count[:, columns], column[...], ratio_rows, plain, scaled)

    terms = gammas[own, :] / new_mult[own, :] * gathered(plain)
    window_total = sum(jnp.sum(mult[...]) for mult in mults)
    logs_out[...] = jnp.log(gathered(scaled) * states / window_total)

    @pl.loop(0, sent.shape[0])
    def _(target):
        sent[target] = terms


def last_kernel(given, state_counts, energy_out, raw_ref):
    depth = energy_out.shape[0]
    states = state_counts.shape[0] * LANES
    number = state_counts.shape[0] // depth
    windows = given.shape[0] // number
    for block in range(number):
        here = slice(block * depth, (block + 1) * depth)
        terms = jnp.sum(given[block * windows : (block + 1) * windows], axis=0)
        raw_ref[here, :] = state_counts[here, :] / terms
    total = jnp.sum(raw_ref[...])
    own = pl.ds(pl.multiple_of(place()[0] * depth, depth), depth)
    energy_out[...] = -jnp.log(raw_ref[own, :] / total * states)


def spot(*shape, dtype=jnp.float32):
    return pltpu.VMEM(shape, dtype)


def keep(x):
    return pltpu.with_memory_space_constraint(x, pltpu.VMEM)


def everyone(block):
    return lax.all_to_all(block, ("frames", "win"), 0, 0, tiled=True)


def call(kernel, ins, outs, scratch=(), scalars=(), limit=16, aliases={}, space=pltpu.VMEM):
    smem = pl.BlockSpec(memory_space=pltpu.SMEM)
    vmem = pl.BlockSpec(memory_space=pltpu.VMEM)
    return pl.pallas_call(
        kernel,
        out_shape=tuple(outs),
        in_specs=[smem] * len(scalars) + [pl.BlockSpec(memory_space=space)] * len(ins),
        out_specs=(vmem,) * len(outs),
        scratch_shapes=list(scratch),
        input_output_aliases=aliases,
        compiler_params=pltpu.CompilerParams(vmem_limit_bytes=limit << 20),
    )(*scalars, *ins)


def estimate(memberships, lag_times, segment_ids, bias_codes):
    frames_dev, states = memberships.shape[1:]
    frames_all = segment_ids.shape[1]
    number = lax.axis_size("frames")
    windows = lax.axis_size("win")
    rows = states // number
    depth = rows // LANES
    group = 2 * rows
    bounds = chunk_bounds(states, group)
    near = 2 * frames_dev
    away = frames_all - near
    half = jnp.bfloat16
    codes = bias_codes.reshape(states // LANES, LANES)
    partner = [(i, i ^ 1) for i in range(number)]
    widths = [high - low for low, high in bounds]
    sizes = [widths[0] + LANES] + widths[1:]
    shapes = [spot(frames_dev, states + LANES, dtype=half)]
    for _ in range(1, number // 2):
        shapes += [spot(frames_dev, width, dtype=half) for width in sizes]
    whole, *parts = call(
        lambda *refs: prepare_kernel(group, *refs),
        [memberships],
        shapes,
        [spot(1, frames_dev, states), pltpu.SemaphoreType.DMA((PIECES,))],
        space=pltpu.HBM,
    )
    route = lambda step: [((i + step) % number, i) for i in range(number)]
    across = []
    for chip in range(1, number // 2):
        across.append([])
        for c in range(len(bounds)):
            across[-1].append(lax.ppermute(parts[(chip - 1) * len(bounds) + c], "frames", route(2 * chip)))
    beside = lax.ppermute(whole, "frames", partner)
    inner, outer, joined, gammas = call(
        lambda *refs: plan_kernel(number, group, *refs),
        [segment_ids, codes],
        [
            spot(near, near, dtype=half),
            spot(max(away, 8), frames_all, dtype=half),
            spot(frames_all, frames_all, dtype=half),
            spot(states // LANES, LANES),
        ],
        [
            spot(1, frames_all, dtype=jnp.int32),
            spot(states // LANES, LANES, dtype=jnp.int32),
            pltpu.SemaphoreType.DMA((2,)),
        ],
        scalars=[lag_times],
        space=pltpu.HBM,
    )
    counts = call(
        lambda *refs: near_kernel(bounds, *refs),
        [whole, beside, keep(inner)],
        [spot(rows, width) for width in widths],
        [spot(2 * near, states, dtype=half), spot(rows, 2 * near, dtype=half)],
    )
    counts = list(counts)
    mults = []
    state = [outer, joined] if away else [joined]
    for c, width in enumerate(widths):
        first, last = c == 0, c == len(bounds) - 1
        blocks = [whole, beside]
        for chunk in across:
            arrived = chunk[c]
            if c:
                arrived, state[0] = lax.optimization_barrier((arrived, state[0]))
            blocks += [arrived, lax.ppermute(arrived, "frames", partner)]
        outs = [spot(rows, width), spot(width // LANES, LANES)]
        sums = [spot(rows, LANES), spot(rows, LANES)]
        scratch = []
        if last:
            outs += [spot(number * windows, 2 * depth, LANES)]
            scratch += sums
        else:
            outs += sums
        if first:
            fixed = [spot(rows, LANES), spot(rows, 2 * max(away, 8), dtype=half), spot(48 + away, frames_all, dtype=half)]
            if last:
                scratch += fixed
            else:
                outs += fixed
        scratch += [spot(2 * max(away, 8), width, dtype=half), spot(width // LANES, LANES)]
        results = call(
            lambda *refs, c=c: counts_kernel(bounds, c, number, *refs),
            [keep(gammas), keep(counts[c])] + blocks + [keep(x) for x in state],
            outs,
            scratch,
            aliases={1: 0},
        )
        counts[c] = results[0]
        mults.append(results[1])
        if not last:
            if first:
                fixed = list(results[4:7]) + [results[1]]
            state = list(results[2:4]) + fixed
    sent = results[2]
    given = everyone(sent)
    sums = [spot(states // LANES, LANES)] * 2 + [spot(rows, LANES)] * 3
    sent, logs, state_counts = call(
        lambda *refs: second_kernel(bounds, *refs),
        [given, keep(gammas)] + [keep(x) for x in mults + counts],
        [spot(number * windows, depth, LANES), spot(depth, LANES), spot(states // LANES, LANES)],
        sums,
    )
    given = everyone(sent)
    (energy,) = call(last_kernel, [given, keep(state_counts)], [spot(depth, LANES)], [spot(states // LANES, LANES)])
    return energy.reshape(rows), logs.reshape(1, rows)


def solution(mesh):
    placed = (P("win", "frames", None), P("win"), P("win", None), P("win", None))
    return jax.shard_map(
        estimate,
        mesh=mesh,
        in_specs=placed,
        out_specs=(P("frames"), P("win", "frames")),
        check_vma=False,
    )
```

time: 148 us -> 61.7 us (0.42)
  blocking collectives: 59.6 us -> 15.2 us
  other arithmetic: 25.5 us -> 0 us
  Pallas kernels: 0 us -> 18.2 us
  matrix products: 15.9 us -> 0 us
  between operations: 14.8 us -> 1.38 us
  waiting for transfers between devices: 26.2 us -> 15.2 us
  starting transfers between devices: 1.33 us -> 7.66 us
    psum x2 -> x0, blocking collectives: 38.7 us -> none  [the longest x1 21.6 us: shards(): count_rows = lax.psum(mult_rows, 'win')]
    all_gather x1 -> x0, waiting for transfers between devices: 25.7 us -> none  [shards(): lax.all_gather(extended, 'frames', axis=0, tiled=True)]
    all_gather x4 -> x0, blocking collectives: 20.8 us -> none  [the longest x1 5.21 us: shards(): mult_full = lax.all_gather(mult_rows, 'frames', axis=0, tiled=True)]
    pallas_call x0 -> x7, Pallas kernels: none -> 18.2 us  [call(): pl.pallas_call(kernel, out_shape=tuple(outs), in_specs=[smem] * len(scala...]
    reduce_sum x5 -> x0, other arithmetic: 17 us -> none  [the longest x1 8.98 us: shards(): new_rows = mult_rows * jnp.sum(ratios * scaled[None, :], axis=1)]
    dot_general x2 -> x0, matrix products: 15.9 us -> none  [the longest x1 8.12 us: add_pair(): jnp.einsum('tr,ts->rs', current_cols, later, preferred_element_type=jnp.f...]
    all_to_all x0 -> x1, blocking collectives: none -> 15.2 us  [everyone(): return lax.all_to_all(block, ('frames', 'win'), 0, 0, tiled=True)]
    ppermute x1 -> x5, waiting for transfers between devices: 0.56 us -> 7.97 us  [the longest x2 6.66 us: estimate(): lax.ppermute(parts[(chip - 1) * len(bounds) + c], 'frames', route(2 * chip))]
  transfers between devices with their start and end apart: 2 -> 6, of which waited for: 2 -> 3; matrix products, arithmetic and copies ran while one was open for 2% -> 1% of each run, Pallas kernels for 0% -> 14%
where the time goes in v2:
time: 61.7 us; the launch traced here: 61.4 us
  Pallas kernels  18.2 us (29%)
  waiting for transfers between devices  15.2 us (25%)
  blocking collectives  15.2 us (25%)
  starting transfers between devices  7.66 us (12%)
  local copies, waits for them, and re-layouts  3.81 us (6%)
  between operations  1.38 us (2%)
    pallas_call x7, Pallas kernels, call(): pl.pallas_call(kernel, out_shape=tuple(outs), in_specs=[smem] * len(scala...  18.2 us
    all_to_all x1, blocking collectives, everyone(): return lax.all_to_all(block, ('frames', 'win'), 0, 0, tiled=True)  15.2 us
    all_to_all x1, waiting for transfers between devices, everyone(): return lax.all_to_all(block, ('frames', 'win'), 0, 0, tiled=True)  7.21 us
    ppermute x2, waiting for transfers between devices, estimate(): lax.ppermute(parts[(chip - 1) * len(bounds) + c], 'frames', route(2 * chip))  6.66 us
    ppermute x2, starting transfers between devices, estimate(): lax.ppermute(parts[(chip - 1) * len(bounds) + c], 'frames', route(2 * chip))  4.8 us
    unnamed x8, local copies, waits for them, and re-layouts  3.81 us
    all_to_all x1, starting transfers between devices, everyone(): return lax.all_to_all(block, ('frames', 'win'), 0, 0, tiled=True)  2.56 us
    ppermute x2, waiting for transfers between devices, estimate(): blocks += [arrived, lax.ppermute(arrived, 'frames', partner)]  1.31 us
  transfers between devices with their start and end apart: 6, of which 3 were waited for; matrix products, arithmetic and copies ran while one was open for 1% of the time, Pallas kernels for 14%

profile of v2, /device:TPU:0, one launch (start us, length us, event | category | flops | bytes accessed | tf_op | source)
XLA Modules:
  0.0 61.4 jit_solution(3094185942346399387)
XLA Ops:
  0.6 0.0 copy-start
  0.6 1.2 %copy-done = f32[1,64,4096]{2,1,0:T(8,128)S(1)} copy-done((f32[1,64,4096]{2,1,0:T(8,128)S(1)}, f32[1,64,4096]{2,1,0:T(8,128)}, u32[]{:S(2)}) %copy-start) | copy-done | bytes 1048600
  1.9 0.3 shard_map.60
  2.2 3.1 %collective-permute-start.2 = (bf16[64,2176]{1,0:T(8,128)(2,1)S(1)}, bf16[64,2176]{1,0:T(8,128)(2,1)S(1)}, u32[]{:S(2)}, u32[]{:S(2)}) collective-permute-start(bf16[64,2176]{1,0:T(8,128)(2,1)S(1)} %get-tuple-element.32), channel_id=1, source_target_pairs={{16,0},{24,8},{0,16},{8,24},{17,1},{25,9},{1,17},{9,25},{18,2},{26... | collective-permute-start | bytes 835592 | tf_op jit(solution)/shard_map/ppermute | solution.py:404
  5.2 0.0 collective-permute-start
  5.2 6.7 %collective-permute-done.2.refs_4_ = bf16[64,2176]{1,0:T(8,128)(2,1)S(1)} collective-permute-done((bf16[64,2176]{1,0:T(8,128)(2,1)S(1)}, bf16[64,2176]{1,0:T(8,128)(2,1)S(1)}, u32[]{:S(2)}, u32[]{:S(2)}) %collective-permute-start.2) | collective-permute-done | bytes 278560 | tf_op jit(solution)/shard_map/ppermute | solution.py:404
  11.9 0.0 collective-permute-start.3
  11.9 1.7 %collective-permute-start.1 = (bf16[64,2048]{1,0:T(8,128)(2,1)S(1)}, bf16[64,2048]{1,0:T(8,128)(2,1)S(1)}, u32[]{:S(2)}, u32[]{:S(2)}) collective-permute-start(bf16[64,2048]{1,0:T(8,128)(2,1)S(1)} %get-tuple-element.30), channel_id=1, source_target_pairs={{16,0},{24,8},{0,16},{8,24},{17,1},{25,9},{1,17},{9,25},{18,2},{26... | collective-permute-start | bytes 786440 | tf_op jit(solution)/shard_map/ppermute | solution.py:404
  14.3 0.0 copy-start.1
  14.3 0.7 %copy-done.1 = s32[1,4096]{1,0:T(1,128)S(1)} copy-done((s32[1,4096]{1,0:T(1,128)S(1)}, s32[1,4096]{1,0:T(1,128)}, u32[]{:S(2)}) %copy-start.1) | copy-done | bytes 16408
  15.0 0.0 copy-start.2
  15.0 0.7 %copy-done.2 = s32[1,256]{1,0:T(1,128)S(1)} copy-done((s32[1,256]{1,0:T(1,128)S(1)}, s32[1,256]{1,0:T(1,128)}, u32[]{:S(2)}) %copy-start.2) | copy-done | bytes 1048
  15.7 0.4 shard_map.59
  16.1 0.0 collective-permute-done.refs_1_.refs_3_
  16.1 4.1 %shard_map.61 = (f32[1024,2048]{1,0:T(8,128)S(1)}, f32[1024,2048]{1,0:T(8,128)S(1)}) custom-call(bf16[64,4224]{1,0:T(8,128)(2,1)S(1)} %get-tuple-element.27.refs_0_.refs_2_, bf16[64,4224]{1,0:T(8,128)(2,1)S(1)} %collective-permute-done.refs_1_.refs_3_, bf16[128,128]{1,0:T(8,128)(2,1)S(1)} %get-tuple-element.28.refs_2_), custom_call_target="tpu_custom_call" | custom-call | tf_op jit(solution)/shard_map/pallas_call | solution.py:362
  20.2 0.0 collective-permute-done.3.refs_5_
  20.2 4.2 %shard_map.62 = (f32[1024,2048]{1,0:T(8,128)S(1)}, f32[16,128]{1,0:T(8,128)S(1)}, f32[1024,128]{1,0:T(8,128)S(1)}, f32[1024,128]{1,0:T(8,128)S(1)}, f32[1024,128...) custom-call(f32[32,128]{1,0:T(8,128)S(1)} %get-tuple-element.26.refs, ...), custom_call_target="tpu_custom_call", output_to_operand_aliasing={{0}: (1, {})} | custom-call | tf_op jit(solution)/shard_map/pallas_call | solution.py:362
  24.4 0.0 collective-permute-done.1.refs_4_
  24.4 0.3 collective-permute-start.4
  24.7 1.3 %collective-permute-done.4.refs_5_ = bf16[64,2048]{1,0:T(8,128)(2,1)S(1)} collective-permute-done((bf16[64,2048]{1,0:T(8,128)(2,1)S(1)}, bf16[64,2048]{1,0:T(8,128)(2,1)S(1)}, u32[]{:S(2)}, u32[]{:S(2)}) %collective-permute-start.4) | collective-permute-done | bytes 262176 | tf_op jit(solution)/shard_map/ppermute | solution.py:439
  26.0 4.2 %shard_map.63 = (f32[1024,2048]{1,0:T(8,128)S(1)}, f32[16,128]{1,0:T(8,128)S(1)}, f32[32,16,128]{2,1,0:T(8,128)S(1)}) custom-call(f32[32,128]{1,0:T(8,128)S(1)} %get-tuple-element.26.refs_0_.refs_1_, f32[1024,2048]{1,0:T(8,128)S(1)} %get-tuple-element.29.refs_1_, ...), custom_call_target="tpu_custom_call", output_to_operand_aliasing={{0}: (1, {})} | custom-call | tf_op jit(solution)/shard_map/pallas_call | solution.py:362
  30.2 15.2 %all_to_all.10.refs_0_ = f32[32,16,128]{2,1,0:T(8,128)S(1)} all-to-all(f32[32,16,128]{2,1,0:T(8,128)S(1)} %get-tuple-element.43), channel_id=1, replica_groups=mesh['frames'=4,'win'=8] {'frames','win'}, dimensions={0} | all-to-all | bytes 524288 | tf_op jit(solution)/shard_map/all_to_all | solution.py:356
  45.4 4.9 %shard_map.64 = (f32[32,8,128]{2,1,0:T(8,128)}, f32[8,128]{1,0:T(8,128)S(1)}, f32[32,128]{1,0:T(8,128)S(1)}) custom-call(f32[32,16,128]{2,1,0:T(8,128)S(1)} %all_to_all.10.refs_0_, f32[32,128]{1,0:T(8,128)S(1)} %get-tuple-element.26.refs_0_.refs_1_, f32[16,128]{1,0:T(8,128)S(1)} %get-tuple-element.42.refs_11_.refs_2_, ...), custom_call_target="tpu_custom_call" | custom-call | tf_op jit(solution)/shard_map/pallas_call | solution.py:362
  50.3 2.6 %all-to-all-start.1 = ((f32[32,8,128]{2,1,0:T(8,128)}), f32[32,8,128]{2,1,0:T(8,128)S(1)}, u32[]{:S(2)}, u32[]{:S(2)}) async-start(f32[32,8,128]{2,1,0:T(8,128)} %get-tuple-element.47), calls=%async_computation.1 | async-start | bytes 262144 | tf_op jit(solution)/shard_map/all_to_all | solution.py:356
  52.9 0.6 copy.11
  53.4 7.2 %all-to-all-done.1.given = f32[32,8,128]{2,1,0:T(8,128)S(1)} async-done(((f32[32,8,128]{2,1,0:T(8,128)}), f32[32,8,128]{2,1,0:T(8,128)S(1)}, u32[]{:S(2)}, u32[]{:S(2)}) %all-to-all-start.1) | async-done | bytes 131104 | tf_op jit(solution)/shard_map/all_to_all | solution.py:356
  60.7 0.1 shard_map.65
  60.8 0.6 copy.10
Async XLA Ops:
  0.6 1.2 %copy-start = (f32[1,64,4096]{2,1,0:T(8,128)S(1)}, f32[1,64,4096]{2,1,0:T(8,128)}, u32[]{:S(2)}) copy-start(f32[1,64,4096]{2,1,0:T(8,128)} %refs_0_.2) | copy-start | bytes 3145732
  2.2 9.7 %collective-permute-start.2 = (bf16[64,2176]{1,0:T(8,128)(2,1)S(1)}, bf16[64,2176]{1,0:T(8,128)(2,1)S(1)}, u32[]{:S(2)}, u32[]{:S(2)}) collective-permute-start(bf16[64,2176]{1,0:T(8,128)(2,1)S(1)} %get-tuple-element.32), channel_id=1, source_target_pairs={{16,0},{24,8},{0,16},{8,24},{17,1},{25,9},{1,17},{9,25},{18,2},{26... | collective-permute-start | bytes 835592 | tf_op jit(solution)/shard_map/ppermute | solution.py:404
  5.2 10.8 %collective-permute-start = (bf16[64,4224]{1,0:T(8,128)(2,1)S(1)}, bf16[64,4224]{1,0:T(8,128)(2,1)S(1)}, u32[]{:S(2)}, u32[]{:S(2)}) collective-permute-start(bf16[64,4224]{1,0:T(8,128)(2,1)S(1)} %get-tuple-element.27.refs_0_.refs_2_), channel_id=1, source_target_pairs={{0,8},{8,0},{16,24},{24,16},{1,9},{9,1},{17,25},{25,17},{2,10},{10... | collective-permute-start | bytes 1622024 | tf_op jit(solution)/shard_map/ppermute | solution.py:405
  11.9 8.2 %collective-permute-start.3 = (bf16[64,2176]{1,0:T(8,128)(2,1)S(1)}, bf16[64,2176]{1,0:T(8,128)(2,1)S(1)}, u32[]{:S(2)}, u32[]{:S(2)}) collective-permute-start(bf16[64,2176]{1,0:T(8,128)(2,1)S(1)} %collective-permute-done.2.refs_4_), channel_id=1, source_target_pairs={{0,8},{8,0},{16,24},{24,16},{1,9},{9,1},{17,25},{25,17},{2,10},{10... | collective-permute-start | bytes 835592 | tf_op jit(solution)/shard_map/ppermute | solution.py:439
  11.9 12.5 %collective-permute-start.1 = (bf16[64,2048]{1,0:T(8,128)(2,1)S(1)}, bf16[64,2048]{1,0:T(8,128)(2,1)S(1)}, u32[]{:S(2)}, u32[]{:S(2)}) collective-permute-start(bf16[64,2048]{1,0:T(8,128)(2,1)S(1)} %get-tuple-element.30), channel_id=1, source_target_pairs={{16,0},{24,8},{0,16},{8,24},{17,1},{25,9},{1,17},{9,25},{18,2},{26... | collective-permute-start | bytes 786440 | tf_op jit(solution)/shard_map/ppermute | solution.py:404
  14.3 0.7 %copy-start.1 = (s32[1,4096]{1,0:T(1,128)S(1)}, s32[1,4096]{1,0:T(1,128)}, u32[]{:S(2)}) copy-start(s32[1,4096]{1,0:T(1,128)} %param.7) | copy-start | bytes 49156
  15.0 0.7 %copy-start.2 = (s32[1,256]{1,0:T(1,128)S(1)}, s32[1,256]{1,0:T(1,128)}, u32[]{:S(2)}) copy-start(s32[1,256]{1,0:T(1,128)} %refs_1_.1) | copy-start | bytes 3076
  24.4 1.6 %collective-permute-start.4 = (bf16[64,2048]{1,0:T(8,128)(2,1)S(1)}, bf16[64,2048]{1,0:T(8,128)(2,1)S(1)}, u32[]{:S(2)}, u32[]{:S(2)}) collective-permute-start(bf16[64,2048]{1,0:T(8,128)(2,1)S(1)} %collective-permute-done.1.refs_4_), channel_id=1, source_target_pairs={{0,8},{8,0},{16,24},{24,16},{1,9},{9,1},{17,25},{25,17},{2,10},{10... | collective-permute-start | bytes 786440 | tf_op jit(solution)/shard_map/ppermute | solution.py:439
  50.3 10.4 %all-to-all-start.1 = ((f32[32,8,128]{2,1,0:T(8,128)}), f32[32,8,128]{2,1,0:T(8,128)S(1)}, u32[]{:S(2)}, u32[]{:S(2)}) async-start(f32[32,8,128]{2,1,0:T(8,128)} %get-tuple-element.47), calls=%async_computation.1 | async-start | bytes 262144 | tf_op jit(solution)/shard_map/all_to_all | solution.py:356

commit v3 on v2

--- a/solution.py
+++ b/solution.py
@@ -9,6 +9,10 @@
 
 
 LANES = 128
+SAFE = 1.0 / 512.0
+BLOCK = 64
+ROWS = 256
+SPAN = 2048
 PIECES = 4
 
 bias_unit = 1.0 / 128.0
@@ -64,15 +68,24 @@
             return tile
 
 
-def add_tile(counts, ratio_col, ratio_rows, plain_ref, scaled_ref):
-    plain = plain_ref[...]
-    scaled = scaled_ref[...]
-    for i, r_row in enumerate(ratio_rows):
-        part = counts[:, i * LANES : (i + 1) * LANES] / (ratio_col + r_row)
-        plain = plain + part
-        scaled = scaled + part * r_row
-    plain_ref[...] = plain
-    scaled_ref[...] = scaled
+def add_tile(counts_of, column, stiff_rows, plain_ref):
+    rows = plain_ref.shape[0]
+    for first in range(0, rows, BLOCK):
+        here = slice(first, first + BLOCK)
+        counts = counts_of(here)
+        stiff_col = column[here, :]
+        plain = plain_ref[here, :]
+        for i, stiff_row in enumerate(stiff_rows):
+            plain = plain + counts[:, i * LANES : (i + 1) * LANES] / (stiff_col + stiff_row)
+        plain_ref[here, :] = plain
+
+
+def add_weighted(count, stiff, first, column, partial):
+    @pl.loop(0, count.shape[1] // LANES)
+    def _(step):
+        columns = pl.ds(pl.multiple_of(step * LANES, LANES), LANES)
+        stiff_row = stiff[pl.ds(first + step, 1), :]
+        partial[...] += count[:, columns] / (column[...] + stiff_row) * stiff_row
 
 
 def place():
@@ -200,20 +213,17 @@
     if is_first:
         outer, joined = take(2) if far else take(1) * 2
     else:
-        plain_in, scaled_in, column, left, outer, mult_own_ref = take(6)
+        plain_in, column, left, outer, earlier_stiff, earlier_mult, earlier_counts = take(7)
     counts_out, mult_out = take(2)
-    if not is_last:
-        plain, scaled = take(2)
-    if is_first and not is_last:
-        column, left, steps = take(3)
-        mult_own_ref = mult_out
     if is_last:
         (sent,) = take(1)
-        plain, scaled = take(2)
-    if is_first and is_last:
+    else:
+        plain, stiff = take(2)
+    if is_first:
         column, left, steps = take(3)
-        mult_own_ref = mult_out
-    pair, ratio = take(2)
+    if is_last:
+        plain, stiff, rest = take(3)
+    (pair,) = take(1)
     frames_dev = blocks[0].shape[0]
     frames_all = number * frames_dev
     away = frames_all - 2 * frames_dev
@@ -246,33 +256,49 @@
         if away:
             pair[:away, j : j + tile] = product[48:].astype(jnp.bfloat16)
             pair[away:, j : j + tile] = jnp.concatenate(others, axis=0)
-    ratio[...] = gammas[low_end // LANES : high_end // LANES, :] * (1.0 / states) / mult_out[...]
+    stiff[...] = mult_out[...] / (gammas[low_end // LANES : high_end // LANES, :] * (1.0 / states))
     if is_first:
         own = pl.ds(pl.multiple_of(core * rows, rows), rows)
         if away:
             left[:, :away] = jnp.transpose(pair[away:, own])
             left[:, away:] = jnp.transpose(pair[:away, own])
-        spread(ratio[own_rows, :], column)
+        spread(stiff[own_rows, :], column)
         plain[...] = jnp.zeros_like(plain)
-        scaled[...] = jnp.zeros_like(scaled)
     else:
         plain[...] = plain_in[...]
-        scaled[...] = scaled_in[...]
-
-    @pl.loop(0, width // tile)
-    def _(step):
-        columns = pl.ds(pl.multiple_of(step * tile, tile), tile)
-        counts = counts_in[:, columns]
-        if away:
-            counts = counts + jnp.dot(left[...], pair[:, columns], preferred_element_type=jnp.float32)
-        counts_out[:, columns] = counts
-        ratio_rows = [ratio[pl.ds(step * (tile // LANES) + i, 1), :] for i in range(tile // LANES)]
-        add_tile(counts, column[...], ratio_rows, plain, scaled)
+
+    for low in range(0, width, tile):
+        columns = slice(low, low + tile)
+        product = jnp.dot(left[...], pair[:, columns], preferred_element_type=jnp.float32) if away else None
+
+        def counts_of(here):
+            counts = counts_in[here, columns]
+            if away:
+                counts = counts + product[here]
+            counts_out[here, columns] = counts
+            return counts
+
+        stiff_rows = [stiff[i : i + 1, :] for i in range(low // LANES, (low + tile) // LANES)]
+        add_tile(counts_of, column, stiff_rows, plain)
 
     if is_last:
-        mult_own = mult_own_ref[own_rows, :]
-        terms = gammas[own_rows, :] / mult_own * gathered(plain)
-        odds = gathered(scaled) * states / terms
+        own_mult_ref, own_stiff_ref = (mult_out, stiff) if is_first else (earlier_mult, earlier_stiff)
+        mult_own = own_mult_ref[own_rows, :]
+        new = own_stiff_ref[own_rows, :] * gathered(plain)
+        stiff_refs = [stiff] if is_first else [earlier_stiff, stiff]
+        counts_refs = [counts_out] if is_first else [earlier_counts, counts_out]
+        whole = mult_own * 2.0
+        rest[...] = whole - new
+
+        @pl.when(jnp.min(rest[...] / whole) < SAFE)
+        def _():
+            plain[...] = jnp.zeros_like(plain)
+            for count, stiff_ref in zip(counts_refs, stiff_refs):
+                add_weighted(count, stiff_ref, 0, column, plain)
+            rest[...] = gathered(plain)
+
+        odds = new / rest[...]
+        terms = rest[...] * states
         windows = sent.shape[0] // number
 
         @pl.loop(0, sent.shape[0])
@@ -286,7 +312,7 @@
     given, gammas = refs[:2]
     mults = refs[2 : 2 + number_chunks]
     counts = refs[2 + number_chunks : 2 + 2 * number_chunks]
-    sent, logs_out, state_counts, new_mult, ratio, column, plain, scaled = refs[2 + 2 * number_chunks :]
+    sent, logs_out, state_counts, new_mult, stiff, column, plain, rest = refs[2 + 2 * number_chunks :]
     depth = logs_out.shape[0]
     states = gammas.shape[0] * LANES
     number = gammas.shape[0] // depth
@@ -302,28 +328,46 @@
         new_mult[here, :] = jnp.sum(jnp.where(own_window, part * others, 0.0), axis=0)
         total = jnp.sum(block_mult, axis=0)
         state_counts[block * depth : (block + 1) * depth, :] = total
-        ratio[here, :] = total / jnp.sum(terms, axis=0)
-    raw = ratio[...]
+        stiff[here, :] = total / jnp.sum(terms, axis=0)
+    raw = stiff[...]
     weights = raw / jnp.sum(raw)
-    ratio[...] = gammas[...] * weights / new_mult[...]
+    stiff[...] = new_mult[...] / (gammas[...] * weights)
     own = pl.ds(pl.multiple_of(core * depth, depth), depth)
-    spread(ratio[own, :], column)
+    weights_own = new_mult[own, :] / (stiff[own, :] * gammas[own, :])
+    spread(stiff[own, :], column)
     plain[...] = jnp.zeros_like(plain)
-    scaled[...] = jnp.zeros_like(scaled)
     for (low_end, high_end), count in zip(bounds, counts):
         width = high_end - low_end
-        tile = column_tile(width)
-
-        @pl.loop(0, width // tile)
-        def _(step):
-            columns = pl.ds(pl.multiple_of(step * tile, tile), tile)
-            start = low_end // LANES + step * (tile // LANES)
-            ratio_rows = [ratio[pl.ds(start + i, 1), :] for i in range(tile // LANES)]
-            add_tile(count[:, columns], column[...], ratio_rows, plain, scaled)
-
-    terms = gammas[own, :] / new_mult[own, :] * gathered(plain)
+        for low in range(0, width, SPAN):
+            span = min(SPAN, width - low)
+            start = (low_end + low) // LANES
+            block = min(ROWS, plain.shape[0])
+
+            @pl.loop(0, plain.shape[0] // block)
+            def _(step):
+                for inner in range(0, block, BLOCK):
+                    here = pl.ds(pl.multiple_of(step * block + inner, BLOCK), BLOCK)
+                    stiff_col = column[here, :]
+                    total = plain[here, :]
+                    for i in range(span // LANES):
+                        cell = count[here, low + i * LANES : low + (i + 1) * LANES]
+                        total = total + cell / (stiff_col + stiff[start + i : start + i + 1, :])
+                    plain[here, :] = total
+
+    whole = mults[0][own, :] * 2.0
+    new = stiff[own, :] * gathered(plain)
+    rest[...] = whole - new
+
+    @pl.when(jnp.min(rest[...] / whole) < SAFE)
+    def _():
+        plain[...] = jnp.zeros_like(plain)
+        for (low_end, _), count in zip(bounds, counts):
+            add_weighted(count, stiff, low_end // LANES, column, plain)
+        rest[...] = gathered(plain)
+
+    terms = rest[...] / weights_own
     window_total = sum(jnp.sum(mult[...]) for mult in mults)
-    logs_out[...] = jnp.log(gathered(scaled) * states / window_total)
+    logs_out[...] = jnp.log(new * states / window_total)
 
     @pl.loop(0, sent.shape[0])
     def _(target):
@@ -438,36 +482,34 @@
                 arrived, state[0] = lax.optimization_barrier((arrived, state[0]))
             blocks += [arrived, lax.ppermute(arrived, "frames", partner)]
         outs = [spot(rows, width), spot(width // LANES, LANES)]
-        sums = [spot(rows, LANES), spot(rows, LANES)]
+        sums = [spot(rows, LANES), spot(width // LANES, LANES)]
         scratch = []
         if last:
             outs += [spot(number * windows, 2 * depth, LANES)]
-            scratch += sums
         else:
             outs += sums
+        fixed = [spot(rows, LANES), spot(rows, 2 * max(away, 8), dtype=half), spot(48 + away, frames_all, dtype=half)]
         if first:
-            fixed = [spot(rows, LANES), spot(rows, 2 * max(away, 8), dtype=half), spot(48 + away, frames_all, dtype=half)]
             if last:
                 scratch += fixed
             else:
                 outs += fixed
-        scratch += [spot(2 * max(away, 8), width, dtype=half), spot(width // LANES, LANES)]
+        if last:
+            scratch += sums + [spot(depth, LANES)]
+        scratch += [spot(2 * max(away, 8), width, dtype=half)]
         results = call(
             lambda *refs, c=c: counts_kernel(bounds, c, number, *refs),
             [keep(gammas), keep(counts[c])] + blocks + [keep(x) for x in state],
             outs,
             scratch,
-            aliases={1: 0},
         )
         counts[c] = results[0]
         mults.append(results[1])
         if not last:
-            if first:
-                fixed = list(results[4:7]) + [results[1]]
-            state = list(results[2:4]) + fixed
+            state = [results[2]] + list(results[4:7]) + [results[3], results[1], results[0]]
     sent = results[2]
     given = everyone(sent)
-    sums = [spot(states // LANES, LANES)] * 2 + [spot(rows, LANES)] * 3
+    sums = [spot(states // LANES, LANES)] * 2 + [spot(rows, LANES)] * 2 + [spot(depth, LANES)]
     sent, logs, state_counts = call(
         lambda *refs: second_kernel(bounds, *refs),
         [given, keep(gammas)] + [keep(x) for x in mults + counts],

time: 61.7 us -> 57.7 us (0.935)
  Pallas kernels: 18.2 us -> 14.2 us
    pallas_call x7, Pallas kernels: 18.2 us -> 14.2 us  [call(): pl.pallas_call(kernel, out_shape=tuple(outs), in_specs=[smem] * len(scala...]
  transfers between devices with their start and end apart: 6 -> 6, of which waited for: 3 -> 3; matrix products, arithmetic and copies ran while one was open for 1% -> 1% of each run, Pallas kernels for 14% -> 13%
where the time goes in v3:
time: 57.7 us; the launch traced here: 57.4 us
  waiting for transfers between devices  15.2 us (26%)
  blocking collectives  15.2 us (26%)
  Pallas kernels  14.2 us (25%)
  starting transfers between devices  7.66 us (13%)
  local copies, waits for them, and re-layouts  3.81 us (7%)
  between operations  1.38 us (2%)
    all_to_all x1, blocking collectives, everyone(): return lax.all_to_all(block, ('frames', 'win'), 0, 0, tiled=True)  15.2 us
    pallas_call x7, Pallas kernels, call(): pl.pallas_call(kernel, out_shape=tuple(outs), in_specs=[smem] * len(scala...  14.2 us
    all_to_all x1, waiting for transfers between devices, everyone(): return lax.all_to_all(block, ('frames', 'win'), 0, 0, tiled=True)  7.21 us
    ppermute x2, waiting for transfers between devices, estimate(): lax.ppermute(parts[(chip - 1) * len(bounds) + c], 'frames', route(2 * chip))  6.66 us
    ppermute x2, starting transfers between devices, estimate(): lax.ppermute(parts[(chip - 1) * len(bounds) + c], 'frames', route(2 * chip))  4.8 us
    unnamed x8, local copies, waits for them, and re-layouts  3.81 us
    all_to_all x1, starting transfers between devices, everyone(): return lax.all_to_all(block, ('frames', 'win'), 0, 0, tiled=True)  2.56 us
    ppermute x2, waiting for transfers between devices, estimate(): blocks += [arrived, lax.ppermute(arrived, 'frames', partner)]  1.31 us
  transfers between devices with their start and end apart: 6, of which 3 were waited for; matrix products, arithmetic and copies ran while one was open for 1% of the time, Pallas kernels for 13%

profile of v3, /device:TPU:0, one launch (start us, length us, event | category | flops | bytes accessed | tf_op | source)
XLA Modules:
  0.0 57.4 jit_solution(17157425579986606475)
XLA Ops:
  0.6 0.0 copy-start
  0.6 1.2 %copy-done = f32[1,64,4096]{2,1,0:T(8,128)S(1)} copy-done((f32[1,64,4096]{2,1,0:T(8,128)S(1)}, f32[1,64,4096]{2,1,0:T(8,128)}, u32[]{:S(2)}) %copy-start) | copy-done | bytes 1048600
  1.9 0.3 shard_map.60
  2.2 3.1 %collective-permute-start.2 = (bf16[64,2176]{1,0:T(8,128)(2,1)S(1)}, bf16[64,2176]{1,0:T(8,128)(2,1)S(1)}, u32[]{:S(2)}, u32[]{:S(2)}) collective-permute-start(bf16[64,2176]{1,0:T(8,128)(2,1)S(1)} %get-tuple-element.32), channel_id=1, source_target_pairs={{16,0},{24,8},{0,16},{8,24},{17,1},{25,9},{1,17},{9,25},{18,2},{26... | collective-permute-start | bytes 835592 | tf_op jit(solution)/shard_map/ppermute | solution.py:448
  5.2 0.0 collective-permute-start
  5.2 6.7 %collective-permute-done.2.refs_4_ = bf16[64,2176]{1,0:T(8,128)(2,1)S(1)} collective-permute-done((bf16[64,2176]{1,0:T(8,128)(2,1)S(1)}, bf16[64,2176]{1,0:T(8,128)(2,1)S(1)}, u32[]{:S(2)}, u32[]{:S(2)}) %collective-permute-start.2) | collective-permute-done | bytes 278560 | tf_op jit(solution)/shard_map/ppermute | solution.py:448
  11.9 0.0 collective-permute-start.3
  11.9 1.7 %collective-permute-start.1 = (bf16[64,2048]{1,0:T(8,128)(2,1)S(1)}, bf16[64,2048]{1,0:T(8,128)(2,1)S(1)}, u32[]{:S(2)}, u32[]{:S(2)}) collective-permute-start(bf16[64,2048]{1,0:T(8,128)(2,1)S(1)} %get-tuple-element.30), channel_id=1, source_target_pairs={{16,0},{24,8},{0,16},{8,24},{17,1},{25,9},{1,17},{9,25},{18,2},{26... | collective-permute-start | bytes 786440 | tf_op jit(solution)/shard_map/ppermute | solution.py:448
  14.3 0.0 copy-start.1
  14.3 0.7 %copy-done.1 = s32[1,4096]{1,0:T(1,128)S(1)} copy-done((s32[1,4096]{1,0:T(1,128)S(1)}, s32[1,4096]{1,0:T(1,128)}, u32[]{:S(2)}) %copy-start.1) | copy-done | bytes 16408
  15.0 0.0 copy-start.2
  15.0 0.7 %copy-done.2 = s32[1,256]{1,0:T(1,128)S(1)} copy-done((s32[1,256]{1,0:T(1,128)S(1)}, s32[1,256]{1,0:T(1,128)}, u32[]{:S(2)}) %copy-start.2) | copy-done | bytes 1048
  15.7 0.4 shard_map.59
  16.1 0.0 collective-permute-done.refs_1_.refs_3_
  16.1 4.1 %shard_map.61 = (f32[1024,2048]{1,0:T(8,128)S(1)}, f32[1024,2048]{1,0:T(8,128)S(1)}) custom-call(bf16[64,4224]{1,0:T(8,128)(2,1)S(1)} %get-tuple-element.27.refs_0_.refs_2_, bf16[64,4224]{1,0:T(8,128)(2,1)S(1)} %collective-permute-done.refs_1_.refs_3_, bf16[128,128]{1,0:T(8,128)(2,1)S(1)} %get-tuple-element.28.refs_2_), custom_call_target="tpu_custom_call" | custom-call | tf_op jit(solution)/shard_map/pallas_call | solution.py:406
  20.2 0.0 collective-permute-done.3.refs_5_
  20.2 2.8 %shard_map.62 = (f32[1024,2048]{1,0:T(8,128)S(1)}, f32[16,128]{1,0:T(8,128)S(1)}, f32[1024,128]{1,0:T(8,128)S(1)}, f32[16,128]{1,0:T(8,128)S(1)}, f32[1024,128]{...) custom-call(f32[32,128]{1,0:T(8,128)S(1)} %get-tuple-element.26.refs_0_.refs_1_, ...), custom_call_target="tpu_custom_call" | custom-call | tf_op jit(solution)/shard_map/pallas_call | solution.py:406
  23.0 0.0 collective-permute-done.1.refs_4_
  23.0 0.3 collective-permute-start.4
  23.3 1.3 %collective-permute-done.4.refs_5_ = bf16[64,2048]{1,0:T(8,128)(2,1)S(1)} collective-permute-done((bf16[64,2048]{1,0:T(8,128)(2,1)S(1)}, bf16[64,2048]{1,0:T(8,128)(2,1)S(1)}, u32[]{:S(2)}, u32[]{:S(2)}) %collective-permute-start.4) | collective-permute-done | bytes 262176 | tf_op jit(solution)/shard_map/ppermute | solution.py:483
  24.6 2.4 %shard_map.63 = (f32[1024,2048]{1,0:T(8,128)S(1)}, f32[16,128]{1,0:T(8,128)S(1)}, f32[32,16,128]{2,1,0:T(8,128)S(1)}) custom-call(f32[32,128]{1,0:T(8,128)S(1)} %get-tuple-element.26.refs_0_.refs_1_, f32[1024,2048]{1,0:T(8,128)S(1)} %get-tuple-element.29.refs_1_, bf16[64,4224]{1,0:T(8,128)(2,1)S(1)} %get-tuple-element.27.refs_0_.refs_2_, ...), custom_call_target="tpu_custom_call" | custom-call | tf_op jit(solution)/shard_map/pallas_call | solution.py:406
  27.0 15.2 %all_to_all.10.refs_0_ = f32[32,16,128]{2,1,0:T(8,128)S(1)} all-to-all(f32[32,16,128]{2,1,0:T(8,128)S(1)} %get-tuple-element.44), channel_id=1, replica_groups=mesh['frames'=4,'win'=8] {'frames','win'}, dimensions={0} | all-to-all | bytes 524288 | tf_op jit(solution)/shard_map/all_to_all | solution.py:400
  42.2 4.1 %shard_map.64 = (f32[32,8,128]{2,1,0:T(8,128)}, f32[8,128]{1,0:T(8,128)S(1)}, f32[32,128]{1,0:T(8,128)S(1)}) custom-call(f32[32,16,128]{2,1,0:T(8,128)S(1)} %all_to_all.10.refs_0_, f32[32,128]{1,0:T(8,128)S(1)} %get-tuple-element.26.refs_0_.refs_1_, f32[16,128]{1,0:T(8,128)S(1)} %get-tuple-element.42.refs_11_.refs_2_, ...), custom_call_target="tpu_custom_call" | custom-call | tf_op jit(solution)/shard_map/pallas_call | solution.py:406
  46.2 2.6 %all-to-all-start.1 = ((f32[32,8,128]{2,1,0:T(8,128)}), f32[32,8,128]{2,1,0:T(8,128)S(1)}, u32[]{:S(2)}, u32[]{:S(2)}) async-start(f32[32,8,128]{2,1,0:T(8,128)} %get-tuple-element.47), calls=%async_computation.1 | async-start | bytes 262144 | tf_op jit(solution)/shard_map/all_to_all | solution.py:400
  48.8 0.6 %copy.7 = f32[1,1024]{1,0:T(1,128)} copy(f32[1,1024]{1,0:T(1,128)S(1)} %bitcast.4) | data formatting | bytes 8192
  49.4 7.2 %all-to-all-done.1.given = f32[32,8,128]{2,1,0:T(8,128)S(1)} async-done(((f32[32,8,128]{2,1,0:T(8,128)}), f32[32,8,128]{2,1,0:T(8,128)S(1)}, u32[]{:S(2)}, u32[]{:S(2)}) %all-to-all-start.1) | async-done | bytes 131104 | tf_op jit(solution)/shard_map/all_to_all | solution.py:400
  56.6 0.1 shard_map.65
  56.8 0.6 %copy.6 = f32[1024]{0:T(1024)} copy(f32[1024]{0:T(1024)S(1)} %bitcast.3) | data formatting | bytes 8192
Async XLA Ops:
  0.6 1.2 %copy-start = (f32[1,64,4096]{2,1,0:T(8,128)S(1)}, f32[1,64,4096]{2,1,0:T(8,128)}, u32[]{:S(2)}) copy-start(f32[1,64,4096]{2,1,0:T(8,128)} %refs_0_.2) | copy-start | bytes 3145732
  2.2 9.7 %collective-permute-start.2 = (bf16[64,2176]{1,0:T(8,128)(2,1)S(1)}, bf16[64,2176]{1,0:T(8,128)(2,1)S(1)}, u32[]{:S(2)}, u32[]{:S(2)}) collective-permute-start(bf16[64,2176]{1,0:T(8,128)(2,1)S(1)} %get-tuple-element.32), channel_id=1, source_target_pairs={{16,0},{24,8},{0,16},{8,24},{17,1},{25,9},{1,17},{9,25},{18,2},{26... | collective-permute-start | bytes 835592 | tf_op jit(solution)/shard_map/ppermute | solution.py:448
  5.2 10.8 %collective-permute-start = (bf16[64,4224]{1,0:T(8,128)(2,1)S(1)}, bf16[64,4224]{1,0:T(8,128)(2,1)S(1)}, u32[]{:S(2)}, u32[]{:S(2)}) collective-permute-start(bf16[64,4224]{1,0:T(8,128)(2,1)S(1)} %get-tuple-element.27.refs_0_.refs_2_), channel_id=1, source_target_pairs={{0,8},{8,0},{16,24},{24,16},{1,9},{9,1},{17,25},{25,17},{2,10},{10... | collective-permute-start | bytes 1622024 | tf_op jit(solution)/shard_map/ppermute | solution.py:449
  11.9 8.3 %collective-permute-start.3 = (bf16[64,2176]{1,0:T(8,128)(2,1)S(1)}, bf16[64,2176]{1,0:T(8,128)(2,1)S(1)}, u32[]{:S(2)}, u32[]{:S(2)}) collective-permute-start(bf16[64,2176]{1,0:T(8,128)(2,1)S(1)} %collective-permute-done.2.refs_4_), channel_id=1, source_target_pairs={{0,8},{8,0},{16,24},{24,16},{1,9},{9,1},{17,25},{25,17},{2,10},{10... | collective-permute-start | bytes 835592 | tf_op jit(solution)/shard_map/ppermute | solution.py:483
  11.9 11.1 %collective-permute-start.1 = (bf16[64,2048]{1,0:T(8,128)(2,1)S(1)}, bf16[64,2048]{1,0:T(8,128)(2,1)S(1)}, u32[]{:S(2)}, u32[]{:S(2)}) collective-permute-start(bf16[64,2048]{1,0:T(8,128)(2,1)S(1)} %get-tuple-element.30), channel_id=1, source_target_pairs={{16,0},{24,8},{0,16},{8,24},{17,1},{25,9},{1,17},{9,25},{18,2},{26... | collective-permute-start | bytes 786440 | tf_op jit(solution)/shard_map/ppermute | solution.py:448
  14.3 0.7 %copy-start.1 = (s32[1,4096]{1,0:T(1,128)S(1)}, s32[1,4096]{1,0:T(1,128)}, u32[]{:S(2)}) copy-start(s32[1,4096]{1,0:T(1,128)} %param.7) | copy-start | bytes 49156
  15.0 0.7 %copy-start.2 = (s32[1,256]{1,0:T(1,128)S(1)}, s32[1,256]{1,0:T(1,128)}, u32[]{:S(2)}) copy-start(s32[1,256]{1,0:T(1,128)} %refs_1_.1) | copy-start | bytes 3076
  23.0 1.6 %collective-permute-start.4 = (bf16[64,2048]{1,0:T(8,128)(2,1)S(1)}, bf16[64,2048]{1,0:T(8,128)(2,1)S(1)}, u32[]{:S(2)}, u32[]{:S(2)}) collective-permute-start(bf16[64,2048]{1,0:T(8,128)(2,1)S(1)} %collective-permute-done.1.refs_4_), channel_id=1, source_target_pairs={{0,8},{8,0},{16,24},{24,16},{1,9},{9,1},{17,25},{25,17},{2,10},{10... | collective-permute-start | bytes 786440 | tf_op jit(solution)/shard_map/ppermute | solution.py:483
  46.2 10.4 %all-to-all-start.1 = ((f32[32,8,128]{2,1,0:T(8,128)}), f32[32,8,128]{2,1,0:T(8,128)S(1)}, u32[]{:S(2)}, u32[]{:S(2)}) async-start(f32[32,8,128]{2,1,0:T(8,128)} %get-tuple-element.47), calls=%async_computation.1 | async-start | bytes 262144 | tf_op jit(solution)/shard_map/all_to_all | solution.py:400

commit v4 on v3

--- a/solution.py
+++ b/solution.py
@@ -86,6 +86,14 @@
         columns = pl.ds(pl.multiple_of(step * LANES, LANES), LANES)
         stiff_row = stiff[pl.ds(first + step, 1), :]
         partial[...] += count[:, columns] / (column[...] + stiff_row) * stiff_row
+
+
+def each(number, put):
+    if number <= 64:
+        for target in range(number):
+            put(target)
+    else:
+        pl.loop(0, number)(put)
 
 
 def place():
@@ -267,6 +275,13 @@
     else:
         plain[...] = plain_in[...]
 
+    if is_last:
+        mult_own = (mult_out if is_first else earlier_mult)[own_rows, :]
+
+        def put_mult(target):
+            sent[target, :depth] = mult_own
+
+        each(sent.shape[0], put_mult)
     for low in range(0, width, tile):
         columns = slice(low, low + tile)
         product = jnp.dot(left[...], pair[:, columns], preferred_element_type=jnp.float32) if away else None
@@ -282,8 +297,7 @@
         add_tile(counts_of, column, stiff_rows, plain)
 
     if is_last:
-        own_mult_ref, own_stiff_ref = (mult_out, stiff) if is_first else (earlier_mult, earlier_stiff)
-        mult_own = own_mult_ref[own_rows, :]
+        own_stiff_ref = stiff if is_first else earlier_stiff
         new = own_stiff_ref[own_rows, :] * gathered(plain)
         stiff_refs = [stiff] if is_first else [earlier_stiff, stiff]
         counts_refs = [counts_out] if is_first else [earlier_counts, counts_out]
@@ -301,10 +315,10 @@
         terms = rest[...] * states
         windows = sent.shape[0] // number
 
-        @pl.loop(0, sent.shape[0])
-        def _(target):
-            sent[target, :depth] = mult_own
+        def put_rest(target):
             sent[target, depth:] = jnp.where(lax.rem(target, windows) == window, odds, terms)
+
+        each(sent.shape[0], put_rest)
 
 
 def second_kernel(bounds, *refs):
@@ -313,7 +327,7 @@
     mults = refs[2 : 2 + number_chunks]
     counts = refs[2 + number_chunks : 2 + 2 * number_chunks]
     sent, logs_out, state_counts, new_mult, stiff, column, plain, rest = refs[2 + 2 * number_chunks :]
-    depth = logs_out.shape[0]
+    depth = logs_out.shape[1] // LANES
     states = gammas.shape[0] * LANES
     number = gammas.shape[0] // depth
     windows = given.shape[0] // number
@@ -367,15 +381,18 @@
 
     terms = rest[...] / weights_own
     window_total = sum(jnp.sum(mult[...]) for mult in mults)
-    logs_out[...] = jnp.log(new * states / window_total)
-
-    @pl.loop(0, sent.shape[0])
-    def _(target):
+    logs = jnp.log(new * states / window_total)
+    for i in range(depth):
+        logs_out[:, i * LANES : (i + 1) * LANES] = logs[i : i + 1, :]
+
+    def put(target):
         sent[target] = terms
 
+    each(sent.shape[0], put)
+
 
 def last_kernel(given, state_counts, energy_out, raw_ref):
-    depth = energy_out.shape[0]
+    depth = energy_out.shape[0] // LANES
     states = state_counts.shape[0] * LANES
     number = state_counts.shape[0] // depth
     windows = given.shape[0] // number
@@ -385,7 +402,9 @@
         raw_ref[here, :] = state_counts[here, :] / terms
     total = jnp.sum(raw_ref[...])
     own = pl.ds(pl.multiple_of(place()[0] * depth, depth), depth)
-    energy_out[...] = -jnp.log(raw_ref[own, :] / total * states)
+    energy = -jnp.log(raw_ref[own, :] / total * states)
+    for i in range(depth):
+        energy_out[i * LANES : (i + 1) * LANES] = energy[i]
 
 
 def spot(*shape, dtype=jnp.float32):
@@ -435,7 +454,7 @@
         shapes += [spot(frames_dev, width, dtype=half) for width in sizes]
     whole, *parts = call(
         lambda *refs: prepare_kernel(group, *refs),
-        [memberships],
+        [pltpu.with_memory_space_constraint(memberships, pltpu.HBM)],
         shapes,
         [spot(1, frames_dev, states), pltpu.SemaphoreType.DMA((PIECES,))],
         space=pltpu.HBM,
@@ -449,7 +468,7 @@
     beside = lax.ppermute(whole, "frames", partner)
     inner, outer, joined, gammas = call(
         lambda *refs: plan_kernel(number, group, *refs),
-        [segment_ids, codes],
+        [pltpu.with_memory_space_constraint(x, pltpu.HBM) for x in (segment_ids, codes)],
         [
             spot(near, near, dtype=half),
             spot(max(away, 8), frames_all, dtype=half),
@@ -513,12 +532,21 @@
     sent, logs, state_counts = call(
         lambda *refs: second_kernel(bounds, *refs),
         [given, keep(gammas)] + [keep(x) for x in mults + counts],
-        [spot(number * windows, depth, LANES), spot(depth, LANES), spot(states // LANES, LANES)],
+        [
+            spot(number * windows, depth, LANES),
+            jax.ShapeDtypeStruct((1, rows), jnp.float32),
+            spot(states // LANES, LANES),
+        ],
         sums,
     )
     given = everyone(sent)
-    (energy,) = call(last_kernel, [given, keep(state_counts)], [spot(depth, LANES)], [spot(states // LANES, LANES)])
-    return energy.reshape(rows), logs.reshape(1, rows)
+    (energy,) = call(
+        last_kernel,
+        [given, keep(state_counts)],
+        [jax.ShapeDtypeStruct((rows,), jnp.float32)],
+        [spot(states // LANES, LANES)],
+    )
+    return energy, logs
 
 
 def solution(mesh):

time: 57.7 us -> 56.2 us (0.974)
  blocking collectives: 15.2 us -> 25.3 us
  waiting for transfers between devices: 15.2 us -> 7.98 us
  local copies, waits for them, and re-layouts: 3.81 us -> 0 us
  starting transfers between devices: 7.66 us -> 5.09 us
  Pallas kernels: 14.2 us -> 16.2 us
    all_to_all x1 -> x2, blocking collectives: 15.2 us -> 25.3 us  [everyone(): return lax.all_to_all(block, ('frames', 'win'), 0, 0, tiled=True)]
    all_to_all x1 -> x0, waiting for transfers between devices: 7.21 us -> none  [everyone(): return lax.all_to_all(block, ('frames', 'win'), 0, 0, tiled=True)]
    unnamed x8 -> x0, local copies, waits for them, and re-layouts: 3.81 us -> none
    all_to_all x1 -> x0, starting transfers between devices: 2.56 us -> none  [everyone(): return lax.all_to_all(block, ('frames', 'win'), 0, 0, tiled=True)]
    pallas_call x7, Pallas kernels: 14.2 us -> 16.2 us  [call(): pl.pallas_call(kernel, out_shape=tuple(outs), in_specs=[smem] * len(scala...]
  transfers between devices with their start and end apart: 6 -> 5, of which waited for: 3 -> 2; matrix products, arithmetic and copies ran while one was open for 1% -> 0% of each run, Pallas kernels for 13% -> 14%
where the time goes in v4:
time: 56.2 us; the launch traced here: 55.8 us
  blocking collectives  25.3 us (45%)
  Pallas kernels  16.2 us (29%)
  waiting for transfers between devices  7.98 us (14%)
  starting transfers between devices  5.09 us (9%)
  between operations  1.34 us (2%)
    all_to_all x2, blocking collectives, everyone(): return lax.all_to_all(block, ('frames', 'win'), 0, 0, tiled=True)  25.3 us
    pallas_call x7, Pallas kernels, call(): pl.pallas_call(kernel, out_shape=tuple(outs), in_specs=[smem] * len(scala...  16.2 us
    ppermute x2, waiting for transfers between devices, estimate(): lax.ppermute(parts[(chip - 1) * len(bounds) + c], 'frames', route(2 * chip))  6.66 us
    ppermute x2, starting transfers between devices, estimate(): lax.ppermute(parts[(chip - 1) * len(bounds) + c], 'frames', route(2 * chip))  4.8 us
    ppermute x2, waiting for transfers between devices, estimate(): blocks += [arrived, lax.ppermute(arrived, 'frames', partner)]  1.32 us
  transfers between devices with their start and end apart: 5, of which 2 were waited for; matrix products, arithmetic and copies ran while one was open for 0% of the time, Pallas kernels for 14%

profile of v4, /device:TPU:0, one launch (start us, length us, event | category | flops | bytes accessed | tf_op | source)
XLA Modules:
  0.0 55.8 jit_solution(1329835278107338786)
XLA Ops:
  0.6 1.4 %shard_map.60 = (bf16[64,4224]{1,0:T(8,128)(2,1)S(1)}, bf16[64,2176]{1,0:T(8,128)(2,1)S(1)}, bf16[64,2048]{1,0:T(8,128)(2,1)S(1)}) custom-call(f32[1,64,4096]{2,1,0:T(8,128)} %refs_0_.2), custom_call_target="tpu_custom_call" | custom-call | tf_op jit(solution)/shard_map/pallas_call | solution.py:425
  2.1 3.1 %collective-permute-start.2 = (bf16[64,2176]{1,0:T(8,128)(2,1)S(1)}, bf16[64,2176]{1,0:T(8,128)(2,1)S(1)}, u32[]{:S(2)}, u32[]{:S(2)}) collective-permute-start(bf16[64,2176]{1,0:T(8,128)(2,1)S(1)} %get-tuple-element.32), channel_id=1, source_target_pairs={{16,0},{24,8},{0,16},{8,24},{17,1},{25,9},{1,17},{9,25},{18,2},{26... | collective-permute-start | bytes 835592 | tf_op jit(solution)/shard_map/ppermute | solution.py:467
  5.1 0.0 collective-permute-start
  5.1 6.7 %collective-permute-done.2.refs_4_ = bf16[64,2176]{1,0:T(8,128)(2,1)S(1)} collective-permute-done((bf16[64,2176]{1,0:T(8,128)(2,1)S(1)}, bf16[64,2176]{1,0:T(8,128)(2,1)S(1)}, u32[]{:S(2)}, u32[]{:S(2)}) %collective-permute-start.2) | collective-permute-done | bytes 278560 | tf_op jit(solution)/shard_map/ppermute | solution.py:467
  11.8 0.0 collective-permute-start.3
  11.8 1.7 %collective-permute-start.1 = (bf16[64,2048]{1,0:T(8,128)(2,1)S(1)}, bf16[64,2048]{1,0:T(8,128)(2,1)S(1)}, u32[]{:S(2)}, u32[]{:S(2)}) collective-permute-start(bf16[64,2048]{1,0:T(8,128)(2,1)S(1)} %get-tuple-element.30), channel_id=1, source_target_pairs={{16,0},{24,8},{0,16},{8,24},{17,1},{25,9},{1,17},{9,25},{18,2},{26... | collective-permute-start | bytes 786440 | tf_op jit(solution)/shard_map/ppermute | solution.py:467
  14.2 1.1 %shard_map.59 = (bf16[128,128]{1,0:T(8,128)(2,1)S(1)}, bf16[128,256]{1,0:T(8,128)(2,1)S(1)}, bf16[256,256]{1,0:T(8,128)(2,1)S(1)}, f32[32,128]{1,0:T(8,128)S(1)}) custom-call(s32[1]{0:T(128)S(6)} %copy.6.refs_0_, s32[1,256]{1,0:T(1,128)} %refs_1_.1, s32[32,128]{1,0:T(8,128)} %bitcast.1), custom_call_target="tpu_custom_call" | custom-call | tf_op jit(solution)/shard_map/pallas_call | solution.py:425
  15.2 0.0 collective-permute-done.refs_1_.refs_3_
  15.3 4.1 %shard_map.61 = (f32[1024,2048]{1,0:T(8,128)S(1)}, f32[1024,2048]{1,0:T(8,128)S(1)}) custom-call(bf16[64,4224]{1,0:T(8,128)(2,1)S(1)} %get-tuple-element.27.refs_0_.refs_2_, bf16[64,4224]{1,0:T(8,128)(2,1)S(1)} %collective-permute-done.refs_1_.refs_3_, bf16[128,128]{1,0:T(8,128)(2,1)S(1)} %get-tuple-element.28.refs_2_), custom_call_target="tpu_custom_call" | custom-call | tf_op jit(solution)/shard_map/pallas_call | solution.py:425
  19.3 0.0 collective-permute-done.3.refs_5_
  19.4 2.8 %shard_map.62 = (f32[1024,2048]{1,0:T(8,128)S(1)}, f32[16,128]{1,0:T(8,128)S(1)}, f32[1024,128]{1,0:T(8,128)S(1)}, f32[16,128]{1,0:T(8,128)S(1)}, f32[1024,128]{...) custom-call(f32[32,128]{1,0:T(8,128)S(1)} %get-tuple-element.26.refs_0_.refs_1_, ...), custom_call_target="tpu_custom_call" | custom-call | tf_op jit(solution)/shard_map/pallas_call | solution.py:425
  22.2 0.0 collective-permute-done.1.refs_4_
  22.2 0.3 collective-permute-start.4
  22.5 1.3 %collective-permute-done.4.refs_5_ = bf16[64,2048]{1,0:T(8,128)(2,1)S(1)} collective-permute-done((bf16[64,2048]{1,0:T(8,128)(2,1)S(1)}, bf16[64,2048]{1,0:T(8,128)(2,1)S(1)}, u32[]{:S(2)}, u32[]{:S(2)}) %collective-permute-start.4) | collective-permute-done | bytes 262176 | tf_op jit(solution)/shard_map/ppermute | solution.py:502
  23.8 2.2 %shard_map.63 = (f32[1024,2048]{1,0:T(8,128)S(1)}, f32[16,128]{1,0:T(8,128)S(1)}, f32[32,16,128]{2,1,0:T(8,128)S(1)}) custom-call(f32[32,128]{1,0:T(8,128)S(1)} %get-tuple-element.26.refs_0_.refs_1_, f32[1024,2048]{1,0:T(8,128)S(1)} %get-tuple-element.29.refs_1_, bf16[64,4224]{1,0:T(8,128)(2,1)S(1)} %get-tuple-element.27.refs_0_.refs_2_, ...), custom_call_target="tpu_custom_call" | custom-call | tf_op jit(solution)/shard_map/pallas_call | solution.py:425
  26.0 15.1 %all_to_all.10.refs_0_ = f32[32,16,128]{2,1,0:T(8,128)S(1)} all-to-all(f32[32,16,128]{2,1,0:T(8,128)S(1)} %get-tuple-element.44), channel_id=1, replica_groups=mesh['frames'=4,'win'=8] {'frames','win'}, dimensions={0} | all-to-all | bytes 524288 | tf_op jit(solution)/shard_map/all_to_all | solution.py:419
  41.1 3.8 %shard_map.64 = (f32[32,8,128]{2,1,0:T(8,128)S(1)}, f32[1,1024]{1,0:T(1,128)}, f32[32,128]{1,0:T(8,128)S(1)}) custom-call(f32[32,16,128]{2,1,0:T(8,128)S(1)} %all_to_all.10.refs_0_, f32[32,128]{1,0:T(8,128)S(1)} %get-tuple-element.26.refs_0_.refs_1_, f32[16,128]{1,0:T(8,128)S(1)} %get-tuple-element.42.refs_11_.refs_2_, ...), custom_call_target="tpu_custom_call" | custom-call | tf_op jit(solution)/shard_map/pallas_call | solution.py:425
  45.0 10.1 %all_to_all.11.given = f32[32,8,128]{2,1,0:T(8,128)S(1)} all-to-all(f32[32,8,128]{2,1,0:T(8,128)S(1)} %get-tuple-element.47), channel_id=1, replica_groups=mesh['frames'=4,'win'=8] {'frames','win'}, dimensions={0} | all-to-all | bytes 262144 | tf_op jit(solution)/shard_map/all_to_all | solution.py:419
  55.1 0.7 %shard_map.65 = f32[1024]{0:T(1024)} custom-call(f32[32,8,128]{2,1,0:T(8,128)S(1)} %all_to_all.11.given, f32[32,128]{1,0:T(8,128)S(1)} %get-tuple-element.48.state_counts), custom_call_target="tpu_custom_call" | custom-call | tf_op jit(solution)/shard_map/pallas_call | solution.py:425
Async XLA Ops:
  2.1 9.7 %collective-permute-start.2 = (bf16[64,2176]{1,0:T(8,128)(2,1)S(1)}, bf16[64,2176]{1,0:T(8,128)(2,1)S(1)}, u32[]{:S(2)}, u32[]{:S(2)}) collective-permute-start(bf16[64,2176]{1,0:T(8,128)(2,1)S(1)} %get-tuple-element.32), channel_id=1, source_target_pairs={{16,0},{24,8},{0,16},{8,24},{17,1},{25,9},{1,17},{9,25},{18,2},{26... | collective-permute-start | bytes 835592 | tf_op jit(solution)/shard_map/ppermute | solution.py:467
  5.1 10.1 %collective-permute-start = (bf16[64,4224]{1,0:T(8,128)(2,1)S(1)}, bf16[64,4224]{1,0:T(8,128)(2,1)S(1)}, u32[]{:S(2)}, u32[]{:S(2)}) collective-permute-start(bf16[64,4224]{1,0:T(8,128)(2,1)S(1)} %get-tuple-element.27.refs_0_.refs_2_), channel_id=1, source_target_pairs={{0,8},{8,0},{16,24},{24,16},{1,9},{9,1},{17,25},{25,17},{2,10},{10... | collective-permute-start | bytes 1622024 | tf_op jit(solution)/shard_map/ppermute | solution.py:468
  11.8 7.6 %collective-permute-start.3 = (bf16[64,2176]{1,0:T(8,128)(2,1)S(1)}, bf16[64,2176]{1,0:T(8,128)(2,1)S(1)}, u32[]{:S(2)}, u32[]{:S(2)}) collective-permute-start(bf16[64,2176]{1,0:T(8,128)(2,1)S(1)} %collective-permute-done.2.refs_4_), channel_id=1, source_target_pairs={{0,8},{8,0},{16,24},{24,16},{1,9},{9,1},{17,25},{25,17},{2,10},{10... | collective-permute-start | bytes 835592 | tf_op jit(solution)/shard_map/ppermute | solution.py:502
  11.8 10.4 %collective-permute-start.1 = (bf16[64,2048]{1,0:T(8,128)(2,1)S(1)}, bf16[64,2048]{1,0:T(8,128)(2,1)S(1)}, u32[]{:S(2)}, u32[]{:S(2)}) collective-permute-start(bf16[64,2048]{1,0:T(8,128)(2,1)S(1)} %get-tuple-element.30), channel_id=1, source_target_pairs={{16,0},{24,8},{0,16},{8,24},{17,1},{25,9},{1,17},{9,25},{18,2},{26... | collective-permute-start | bytes 786440 | tf_op jit(solution)/shard_map/ppermute | solution.py:467
  22.2 1.6 %collective-permute-start.4 = (bf16[64,2048]{1,0:T(8,128)(2,1)S(1)}, bf16[64,2048]{1,0:T(8,128)(2,1)S(1)}, u32[]{:S(2)}, u32[]{:S(2)}) collective-permute-start(bf16[64,2048]{1,0:T(8,128)(2,1)S(1)} %collective-permute-done.1.refs_4_), channel_id=1, source_target_pairs={{0,8},{8,0},{16,24},{24,16},{1,9},{9,1},{17,25},{25,17},{2,10},{10... | collective-permute-start | bytes 786440 | tf_op jit(solution)/shard_map/ppermute | solution.py:502

commit v5 on v4

--- a/solution.py
+++ b/solution.py
@@ -278,8 +278,14 @@
     if is_last:
         mult_own = (mult_out if is_first else earlier_mult)[own_rows, :]
 
+        half = depth // 2
+
+        def half_for(target, block):
+            first = lax.rem(target // (sent.shape[0] // number), 2) == 0
+            return jnp.where(first, block[:half], block[half:])
+
         def put_mult(target):
-            sent[target, :depth] = mult_own
+            sent[target, :half] = half_for(target, mult_own)
 
         each(sent.shape[0], put_mult)
     for low in range(0, width, tile):
@@ -316,33 +322,53 @@
         windows = sent.shape[0] // number
 
         def put_rest(target):
-            sent[target, depth:] = jnp.where(lax.rem(target, windows) == window, odds, terms)
+            own_window = lax.rem(target, windows) == window
+            sent[target, half:] = jnp.where(own_window, half_for(target, odds), half_for(target, terms))
 
         each(sent.shape[0], put_rest)
+
+
+def merge_kernel(number, given, merged):
+    windows = given.shape[0] // number
+    half = given.shape[1] // 2
+    states = number * 2 * half * LANES
+    window = place()[1]
+    own_window = lax.broadcasted_iota(jnp.int32, (windows, half, LANES), 0) == window
+    for block in range(number):
+        here = slice(block * half, (block + 1) * half)
+        block_mult = given[block * windows : (block + 1) * windows, :half]
+        others = given[block * windows : (block + 1) * windows, half:]
+        part = 2.0 * block_mult / (1.0 + others)
+        terms = jnp.where(own_window, part * states, others)
+        total = jnp.sum(block_mult, axis=0)
+        merged[0, here, :] = total / jnp.sum(terms, axis=0)
+        merged[1, here, :] = jnp.sum(jnp.where(own_window, part * others, 0.0), axis=0)
+        merged[2, here, :] = total
 
 
 def second_kernel(bounds, *refs):
     number_chunks = len(bounds)
-    given, gammas = refs[:2]
-    mults = refs[2 : 2 + number_chunks]
-    counts = refs[2 + number_chunks : 2 + 2 * number_chunks]
-    sent, logs_out, state_counts, new_mult, stiff, column, plain, rest = refs[2 + 2 * number_chunks :]
+    merged, beside, gammas = refs[:3]
+    mults = refs[3 : 3 + number_chunks]
+    counts = refs[3 + number_chunks : 3 + 2 * number_chunks]
+    sent, logs_out, state_counts, new_mult, stiff, column, plain, rest = refs[3 + 2 * number_chunks :]
     depth = logs_out.shape[1] // LANES
+    half = depth // 2
     states = gammas.shape[0] * LANES
     number = gammas.shape[0] // depth
-    windows = given.shape[0] // number
-    _, window, core, own_chip = place()
-    own_window = lax.broadcasted_iota(jnp.int32, (windows, depth, LANES), 0) == window
+    _, _, core, own_chip = place()
     for block in range(number):
         here = pl.ds(pl.multiple_of(lax.rem(block + (number - 2 * own_chip), number) * depth, depth), depth)
-        block_mult = given[block * windows : (block + 1) * windows, :depth]
-        others = given[block * windows : (block + 1) * windows, depth:]
-        part = 2.0 * block_mult / (1.0 + others)
-        terms = jnp.where(own_window, part * states, others)
-        new_mult[here, :] = jnp.sum(jnp.where(own_window, part * others, 0.0), axis=0)
-        total = jnp.sum(block_mult, axis=0)
-        state_counts[block * depth : (block + 1) * depth, :] = total
-        stiff[here, :] = total / jnp.sum(terms, axis=0)
+        whole = []
+        for i in range(3):
+            mine = merged[i, block * half : (block + 1) * half, :]
+            theirs = beside[i, block * half : (block + 1) * half, :]
+            whole.append(
+                jnp.concatenate([jnp.where(core == 0, mine, theirs), jnp.where(core == 0, theirs, mine)], axis=0)
+            )
+        stiff[here, :] = whole[0]
+        new_mult[here, :] = whole[1]
+        state_counts[block * depth : (block + 1) * depth, :] = whole[2]
     raw = stiff[...]
     weights = raw / jnp.sum(raw)
     stiff[...] = new_mult[...] / (gammas[...] * weights)
@@ -504,7 +530,7 @@
         sums = [spot(rows, LANES), spot(width // LANES, LANES)]
         scratch = []
         if last:
-            outs += [spot(number * windows, 2 * depth, LANES)]
+            outs += [spot(number * windows, depth, LANES)]
         else:
             outs += sums
         fixed = [spot(rows, LANES), spot(rows, 2 * max(away, 8), dtype=half), spot(48 + away, frames_all, dtype=half)]
@@ -526,12 +552,13 @@
         mults.append(results[1])
         if not last:
             state = [results[2]] + list(results[4:7]) + [results[3], results[1], results[0]]
-    sent = results[2]
-    given = everyone(sent)
+    given = everyone(results[2])
+    (merged,) = call(lambda *refs: merge_kernel(number, *refs), [given], [spot(3, states // LANES // 2, LANES)])
+    beside = lax.ppermute(merged, "frames", partner)
     sums = [spot(states // LANES, LANES)] * 2 + [spot(rows, LANES)] * 2 + [spot(depth, LANES)]
     sent, logs, state_counts = call(
         lambda *refs: second_kernel(bounds, *refs),
-        [given, keep(gammas)] + [keep(x) for x in mults + counts],
+        [merged, beside, keep(gammas)] + [keep(x) for x in mults + counts],
         [
             spot(number * windows, depth, LANES),
             jax.ShapeDtypeStruct((1, rows), jnp.float32),

time: 56.2 us -> 54.5 us (0.970)
  blocking collectives: 25.3 us -> 22.5 us
  waiting for transfers between devices: 7.98 us -> 9.06 us
    all_to_all x2, blocking collectives: 25.3 us -> 22.5 us  [everyone(): return lax.all_to_all(block, ('frames', 'win'), 0, 0, tiled=True)]
    ppermute x0 -> x1, waiting for transfers between devices: none -> 1.08 us  [estimate(): beside = lax.ppermute(merged, 'frames', partner)]
    pallas_call x7 -> x8, Pallas kernels: 16.2 us -> 16.1 us  [call(): pl.pallas_call(kernel, out_shape=tuple(outs), in_specs=[smem] * len(scala...]
  transfers between devices with their start and end apart: 5 -> 6, of which waited for: 2 -> 3; matrix products, arithmetic and copies ran while one was open for 0% -> 0% of each run, Pallas kernels for 14% -> 14%
where the time goes in v5:
time: 54.5 us; the launch traced here: 54.2 us
  blocking collectives  22.5 us (41%)
  Pallas kernels  16.1 us (30%)
  waiting for transfers between devices  9.06 us (17%)
  starting transfers between devices  5.26 us (10%)
  between operations  1.35 us (2%)
    all_to_all x2, blocking collectives, everyone(): return lax.all_to_all(block, ('frames', 'win'), 0, 0, tiled=True)  22.5 us
    pallas_call x8, Pallas kernels, call(): pl.pallas_call(kernel, out_shape=tuple(outs), in_specs=[smem] * len(scala...  16.1 us
    ppermute x2, waiting for transfers between devices, estimate(): lax.ppermute(parts[(chip - 1) * len(bounds) + c], 'frames', route(2 * chip))  6.66 us
    ppermute x2, starting transfers between devices, estimate(): lax.ppermute(parts[(chip - 1) * len(bounds) + c], 'frames', route(2 * chip))  4.8 us
    ppermute x2, waiting for transfers between devices, estimate(): blocks += [arrived, lax.ppermute(arrived, 'frames', partner)]  1.32 us
  transfers between devices with their start and end apart: 6, of which 3 were waited for; matrix products, arithmetic and copies ran while one was open for 0% of the time, Pallas kernels for 14%

profile of v5, /device:TPU:0, one launch (start us, length us, event | category | flops | bytes accessed | tf_op | source)
XLA Modules:
  0.0 54.2 jit_solution(4610128964577406731)
XLA Ops:
  0.6 1.4 %shard_map.60 = (bf16[64,4224]{1,0:T(8,128)(2,1)S(1)}, bf16[64,2176]{1,0:T(8,128)(2,1)S(1)}, bf16[64,2048]{1,0:T(8,128)(2,1)S(1)}) custom-call(f32[1,64,4096]{2,1,0:T(8,128)} %refs_0_.2), custom_call_target="tpu_custom_call" | custom-call | tf_op jit(solution)/shard_map/pallas_call | solution.py:451
  2.1 3.1 %collective-permute-start.2 = (bf16[64,2176]{1,0:T(8,128)(2,1)S(1)}, bf16[64,2176]{1,0:T(8,128)(2,1)S(1)}, u32[]{:S(2)}, u32[]{:S(2)}) collective-permute-start(bf16[64,2176]{1,0:T(8,128)(2,1)S(1)} %get-tuple-element.32), channel_id=1, source_target_pairs={{16,0},{24,8},{0,16},{8,24},{17,1},{25,9},{1,17},{9,25},{18,2},{26... | collective-permute-start | bytes 835592 | tf_op jit(solution)/shard_map/ppermute | solution.py:493
  5.1 0.0 collective-permute-start
  5.1 6.7 %collective-permute-done.2.refs_4_ = bf16[64,2176]{1,0:T(8,128)(2,1)S(1)} collective-permute-done((bf16[64,2176]{1,0:T(8,128)(2,1)S(1)}, bf16[64,2176]{1,0:T(8,128)(2,1)S(1)}, u32[]{:S(2)}, u32[]{:S(2)}) %collective-permute-start.2) | collective-permute-done | bytes 278560 | tf_op jit(solution)/shard_map/ppermute | solution.py:493
  11.8 0.0 collective-permute-start.3
  11.8 1.7 %collective-permute-start.1 = (bf16[64,2048]{1,0:T(8,128)(2,1)S(1)}, bf16[64,2048]{1,0:T(8,128)(2,1)S(1)}, u32[]{:S(2)}, u32[]{:S(2)}) collective-permute-start(bf16[64,2048]{1,0:T(8,128)(2,1)S(1)} %get-tuple-element.30), channel_id=1, source_target_pairs={{16,0},{24,8},{0,16},{8,24},{17,1},{25,9},{1,17},{9,25},{18,2},{26... | collective-permute-start | bytes 786440 | tf_op jit(solution)/shard_map/ppermute | solution.py:493
  14.2 1.1 %shard_map.59 = (bf16[128,128]{1,0:T(8,128)(2,1)S(1)}, bf16[128,256]{1,0:T(8,128)(2,1)S(1)}, bf16[256,256]{1,0:T(8,128)(2,1)S(1)}, f32[32,128]{1,0:T(8,128)S(1)}) custom-call(s32[1]{0:T(128)S(6)} %copy.6.refs_0_, s32[1,256]{1,0:T(1,128)} %refs_1_.1, s32[32,128]{1,0:T(8,128)} %bitcast.1), custom_call_target="tpu_custom_call" | custom-call | tf_op jit(solution)/shard_map/pallas_call | solution.py:451
  15.2 0.0 collective-permute-done.refs_1_.refs_3_
  15.3 4.1 %shard_map.61 = (f32[1024,2048]{1,0:T(8,128)S(1)}, f32[1024,2048]{1,0:T(8,128)S(1)}) custom-call(bf16[64,4224]{1,0:T(8,128)(2,1)S(1)} %get-tuple-element.27.refs_0_.refs_2_, bf16[64,4224]{1,0:T(8,128)(2,1)S(1)} %collective-permute-done.refs_1_.refs_3_, bf16[128,128]{1,0:T(8,128)(2,1)S(1)} %get-tuple-element.28.refs_2_), custom_call_target="tpu_custom_call" | custom-call | tf_op jit(solution)/shard_map/pallas_call | solution.py:451
  19.3 0.0 collective-permute-done.3.refs_5_
  19.4 2.7 %shard_map.62 = (f32[1024,2048]{1,0:T(8,128)S(1)}, f32[16,128]{1,0:T(8,128)S(1)}, f32[1024,128]{1,0:T(8,128)S(1)}, f32[16,128]{1,0:T(8,128)S(1)}, f32[1024,128]{...) custom-call(f32[32,128]{1,0:T(8,128)S(1)} %get-tuple-element.26.refs_0_.refs_2_, ...), custom_call_target="tpu_custom_call" | custom-call | tf_op jit(solution)/shard_map/pallas_call | solution.py:451
  22.0 0.0 collective-permute-done.1.refs_4_
  22.1 0.3 collective-permute-start.4
  22.3 1.3 %collective-permute-done.4.refs_5_ = bf16[64,2048]{1,0:T(8,128)(2,1)S(1)} collective-permute-done((bf16[64,2048]{1,0:T(8,128)(2,1)S(1)}, bf16[64,2048]{1,0:T(8,128)(2,1)S(1)}, u32[]{:S(2)}, u32[]{:S(2)}) %collective-permute-start.4) | collective-permute-done | bytes 262176 | tf_op jit(solution)/shard_map/ppermute | solution.py:528
  23.7 2.2 %shard_map.63 = (f32[1024,2048]{1,0:T(8,128)S(1)}, f32[16,128]{1,0:T(8,128)S(1)}, f32[32,8,128]{2,1,0:T(8,128)S(1)}) custom-call(f32[32,128]{1,0:T(8,128)S(1)} %get-tuple-element.26.refs_0_.refs_2_, f32[1024,2048]{1,0:T(8,128)S(1)} %get-tuple-element.29.refs_1_, bf16[64,4224]{1,0:T(8,128)(2,1)S(1)} %get-tuple-element.27.refs_0_.refs_2_, ...), custom_call_target="tpu_custom_call" | custom-call | tf_op jit(solution)/shard_map/pallas_call | solution.py:451
  25.9 12.5 %all_to_all.10.refs_0_ = f32[32,8,128]{2,1,0:T(8,128)S(1)} all-to-all(f32[32,8,128]{2,1,0:T(8,128)S(1)} %get-tuple-element.44), channel_id=1, replica_groups=mesh['frames'=4,'win'=8] {'frames','win'}, dimensions={0} | all-to-all | bytes 262144 | tf_op jit(solution)/shard_map/all_to_all | solution.py:445
  38.4 0.1 shard_map.64.refs_0_
  38.5 0.2 collective-permute-start.5
  38.6 1.1 %collective-permute-done.5.refs_1_ = f32[3,16,128]{2,1,0:T(8,128)S(1)} collective-permute-done((f32[3,16,128]{2,1,0:T(8,128)S(1)}, f32[3,16,128]{2,1,0:T(8,128)S(1)}, u32[]{:S(2)}, u32[]{:S(2)}) %collective-permute-start.5) | collective-permute-done | bytes 24608 | tf_op jit(solution)/shard_map/ppermute | solution.py:557
  39.7 3.8 %shard_map.65 = (f32[32,8,128]{2,1,0:T(8,128)S(1)}, f32[1,1024]{1,0:T(1,128)}, f32[32,128]{1,0:T(8,128)S(1)}) custom-call(f32[3,16,128]{2,1,0:T(8,128)S(1)} %shard_map.64.refs_0_, f32[3,16,128]{2,1,0:T(8,128)S(1)} %collective-permute-done.5.refs_1_, f32[32,128]{1,0:T(8,128)S(1)} %get-tuple-element.26.refs_0_.refs_2_, ...), custom_call_target="tpu_custom_call" | custom-call | tf_op jit(solution)/shard_map/pallas_call | solution.py:451
  43.5 10.0 %all_to_all.11.given = f32[32,8,128]{2,1,0:T(8,128)S(1)} all-to-all(f32[32,8,128]{2,1,0:T(8,128)S(1)} %get-tuple-element.47), channel_id=1, replica_groups=mesh['frames'=4,'win'=8] {'frames','win'}, dimensions={0} | all-to-all | bytes 262144 | tf_op jit(solution)/shard_map/all_to_all | solution.py:445
  53.5 0.7 %shard_map.66 = f32[1024]{0:T(1024)} custom-call(f32[32,8,128]{2,1,0:T(8,128)S(1)} %all_to_all.11.given, f32[32,128]{1,0:T(8,128)S(1)} %get-tuple-element.48.state_counts), custom_call_target="tpu_custom_call" | custom-call | tf_op jit(solution)/shard_map/pallas_call | solution.py:451
Async XLA Ops:
  2.1 9.7 %collective-permute-start.2 = (bf16[64,2176]{1,0:T(8,128)(2,1)S(1)}, bf16[64,2176]{1,0:T(8,128)(2,1)S(1)}, u32[]{:S(2)}, u32[]{:S(2)}) collective-permute-start(bf16[64,2176]{1,0:T(8,128)(2,1)S(1)} %get-tuple-element.32), channel_id=1, source_target_pairs={{16,0},{24,8},{0,16},{8,24},{17,1},{25,9},{1,17},{9,25},{18,2},{26... | collective-permute-start | bytes 835592 | tf_op jit(solution)/shard_map/ppermute | solution.py:493
  5.1 10.1 %collective-permute-start = (bf16[64,4224]{1,0:T(8,128)(2,1)S(1)}, bf16[64,4224]{1,0:T(8,128)(2,1)S(1)}, u32[]{:S(2)}, u32[]{:S(2)}) collective-permute-start(bf16[64,4224]{1,0:T(8,128)(2,1)S(1)} %get-tuple-element.27.refs_0_.refs_2_), channel_id=1, source_target_pairs={{0,8},{8,0},{16,24},{24,16},{1,9},{9,1},{17,25},{25,17},{2,10},{10... | collective-permute-start | bytes 1622024 | tf_op jit(solution)/shard_map/ppermute | solution.py:494
  11.8 7.6 %collective-permute-start.3 = (bf16[64,2176]{1,0:T(8,128)(2,1)S(1)}, bf16[64,2176]{1,0:T(8,128)(2,1)S(1)}, u32[]{:S(2)}, u32[]{:S(2)}) collective-permute-start(bf16[64,2176]{1,0:T(8,128)(2,1)S(1)} %collective-permute-done.2.refs_4_), channel_id=1, source_target_pairs={{0,8},{8,0},{16,24},{24,16},{1,9},{9,1},{17,25},{25,17},{2,10},{10... | collective-permute-start | bytes 835592 | tf_op jit(solution)/shard_map/ppermute | solution.py:528
  11.8 10.3 %collective-permute-start.1 = (bf16[64,2048]{1,0:T(8,128)(2,1)S(1)}, bf16[64,2048]{1,0:T(8,128)(2,1)S(1)}, u32[]{:S(2)}, u32[]{:S(2)}) collective-permute-start(bf16[64,2048]{1,0:T(8,128)(2,1)S(1)} %get-tuple-element.30), channel_id=1, source_target_pairs={{16,0},{24,8},{0,16},{8,24},{17,1},{25,9},{1,17},{9,25},{18,2},{26... | collective-permute-start | bytes 786440 | tf_op jit(solution)/shard_map/ppermute | solution.py:493
  22.1 1.6 %collective-permute-start.4 = (bf16[64,2048]{1,0:T(8,128)(2,1)S(1)}, bf16[64,2048]{1,0:T(8,128)(2,1)S(1)}, u32[]{:S(2)}, u32[]{:S(2)}) collective-permute-start(bf16[64,2048]{1,0:T(8,128)(2,1)S(1)} %collective-permute-done.1.refs_4_), channel_id=1, source_target_pairs={{0,8},{8,0},{16,24},{24,16},{1,9},{9,1},{17,25},{25,17},{2,10},{10... | collective-permute-start | bytes 786440 | tf_op jit(solution)/shard_map/ppermute | solution.py:528
  38.5 1.3 %collective-permute-start.5 = (f32[3,16,128]{2,1,0:T(8,128)S(1)}, f32[3,16,128]{2,1,0:T(8,128)S(1)}, u32[]{:S(2)}, u32[]{:S(2)}) collective-permute-start(f32[3,16,128]{2,1,0:T(8,128)S(1)} %shard_map.64.refs_0_), channel_id=1, source_target_pairs={{0,8},{8,0},{16,24},{24,16},{1,9},{9,1},{17,25},{25,17},{2,10},{10... | collective-permute-start | bytes 73736 | tf_op jit(solution)/shard_map/ppermute | solution.py:557

commit v6 on v5

--- a/solution.py
+++ b/solution.py
@@ -352,7 +352,7 @@
     mults = refs[3 : 3 + number_chunks]
     counts = refs[3 + number_chunks : 3 + 2 * number_chunks]
     sent, logs_out, state_counts, new_mult, stiff, column, plain, rest = refs[3 + 2 * number_chunks :]
-    depth = logs_out.shape[1] // LANES
+    depth = logs_out.shape[0]
     half = depth // 2
     states = gammas.shape[0] * LANES
     number = gammas.shape[0] // depth
@@ -407,9 +407,7 @@
 
     terms = rest[...] / weights_own
     window_total = sum(jnp.sum(mult[...]) for mult in mults)
-    logs = jnp.log(new * states / window_total)
-    for i in range(depth):
-        logs_out[:, i * LANES : (i + 1) * LANES] = logs[i : i + 1, :]
+    logs_out[...] = jnp.log(new * states / window_total)
 
     def put(target):
         sent[target] = terms
@@ -417,7 +415,9 @@
     each(sent.shape[0], put)
 
 
-def last_kernel(given, state_counts, energy_out, raw_ref):
+def last_kernel(given, state_counts, logs, energy_out, logs_out, raw_ref):
+    for i in range(logs.shape[0]):
+        logs_out[:, i * LANES : (i + 1) * LANES] = logs[i : i + 1, :]
     depth = energy_out.shape[0] // LANES
     states = state_counts.shape[0] * LANES
     number = state_counts.shape[0] // depth
@@ -561,16 +561,16 @@
         [merged, beside, keep(gammas)] + [keep(x) for x in mults + counts],
         [
             spot(number * windows, depth, LANES),
-            jax.ShapeDtypeStruct((1, rows), jnp.float32),
+            spot(depth, LANES),
             spot(states // LANES, LANES),
         ],
         sums,
     )
     given = everyone(sent)
-    (energy,) = call(
+    energy, logs = call(
         last_kernel,
-        [given, keep(state_counts)],
-        [jax.ShapeDtypeStruct((rows,), jnp.float32)],
+        [given, keep(state_counts), keep(logs)],
+        [jax.ShapeDtypeStruct((rows,), jnp.float32), jax.ShapeDtypeStruct((1, rows), jnp.float32)],
         [spot(states // LANES, LANES)],
     )
     return energy, logs

time: 54.5 us -> 53.9 us (0.989)
  Pallas kernels: 16.1 us -> 15.5 us
    pallas_call x8, Pallas kernels: 16.1 us -> 15.5 us  [call(): pl.pallas_call(kernel, out_shape=tuple(outs), in_specs=[smem] * len(scala...]
  transfers between devices with their start and end apart: 6 -> 6, of which waited for: 3 -> 3; matrix products, arithmetic and copies ran while one was open for 0% -> 0% of each run, Pallas kernels for 14% -> 15%
where the time goes in v6:
time: 53.9 us; the launch traced here: 53.6 us
  blocking collectives  22.5 us (42%)
  Pallas kernels  15.5 us (29%)
  waiting for transfers between devices  9.06 us (17%)
  starting transfers between devices  5.26 us (10%)
  between operations  1.35 us (3%)
    all_to_all x2, blocking collectives, everyone(): return lax.all_to_all(block, ('frames', 'win'), 0, 0, tiled=True)  22.5 us
    pallas_call x8, Pallas kernels, call(): pl.pallas_call(kernel, out_shape=tuple(outs), in_specs=[smem] * len(scala...  15.5 us
    ppermute x2, waiting for transfers between devices, estimate(): lax.ppermute(parts[(chip - 1) * len(bounds) + c], 'frames', route(2 * chip))  6.66 us
    ppermute x2, starting transfers between devices, estimate(): lax.ppermute(parts[(chip - 1) * len(bounds) + c], 'frames', route(2 * chip))  4.8 us
    ppermute x2, waiting for transfers between devices, estimate(): blocks += [arrived, lax.ppermute(arrived, 'frames', partner)]  1.32 us
    ppermute x1, waiting for transfers between devices, estimate(): beside = lax.ppermute(merged, 'frames', partner)  1.08 us
  transfers between devices with their start and end apart: 6, of which 3 were waited for; matrix products, arithmetic and copies ran while one was open for 0% of the time, Pallas kernels for 15%

profile of v6, /device:TPU:0, one launch (start us, length us, event | category | flops | bytes accessed | tf_op | source)
XLA Modules:
  0.0 53.6 jit_solution(12359672006473664638)
XLA Ops:
  0.6 1.4 %shard_map.60 = (bf16[64,4224]{1,0:T(8,128)(2,1)S(1)}, bf16[64,2176]{1,0:T(8,128)(2,1)S(1)}, bf16[64,2048]{1,0:T(8,128)(2,1)S(1)}) custom-call(f32[1,64,4096]{2,1,0:T(8,128)} %refs_0_.2), custom_call_target="tpu_custom_call" | custom-call | tf_op jit(solution)/shard_map/pallas_call | solution.py:451
  2.1 3.1 %collective-permute-start.2 = (bf16[64,2176]{1,0:T(8,128)(2,1)S(1)}, bf16[64,2176]{1,0:T(8,128)(2,1)S(1)}, u32[]{:S(2)}, u32[]{:S(2)}) collective-permute-start(bf16[64,2176]{1,0:T(8,128)(2,1)S(1)} %get-tuple-element.32), channel_id=1, source_target_pairs={{16,0},{24,8},{0,16},{8,24},{17,1},{25,9},{1,17},{9,25},{18,2},{26... | collective-permute-start | bytes 835592 | tf_op jit(solution)/shard_map/ppermute | solution.py:493
  5.1 0.0 collective-permute-start
  5.1 6.7 %collective-permute-done.2.refs_4_ = bf16[64,2176]{1,0:T(8,128)(2,1)S(1)} collective-permute-done((bf16[64,2176]{1,0:T(8,128)(2,1)S(1)}, bf16[64,2176]{1,0:T(8,128)(2,1)S(1)}, u32[]{:S(2)}, u32[]{:S(2)}) %collective-permute-start.2) | collective-permute-done | bytes 278560 | tf_op jit(solution)/shard_map/ppermute | solution.py:493
  11.8 0.0 collective-permute-start.3
  11.8 1.7 %collective-permute-start.1 = (bf16[64,2048]{1,0:T(8,128)(2,1)S(1)}, bf16[64,2048]{1,0:T(8,128)(2,1)S(1)}, u32[]{:S(2)}, u32[]{:S(2)}) collective-permute-start(bf16[64,2048]{1,0:T(8,128)(2,1)S(1)} %get-tuple-element.30), channel_id=1, source_target_pairs={{16,0},{24,8},{0,16},{8,24},{17,1},{25,9},{1,17},{9,25},{18,2},{26... | collective-permute-start | bytes 786440 | tf_op jit(solution)/shard_map/ppermute | solution.py:493
  14.2 1.1 %shard_map.59 = (bf16[128,128]{1,0:T(8,128)(2,1)S(1)}, bf16[128,256]{1,0:T(8,128)(2,1)S(1)}, bf16[256,256]{1,0:T(8,128)(2,1)S(1)}, f32[32,128]{1,0:T(8,128)S(1)}) custom-call(s32[1]{0:T(128)S(6)} %copy.6.refs_0_, s32[1,256]{1,0:T(1,128)} %refs_1_.1, s32[32,128]{1,0:T(8,128)} %bitcast.1), custom_call_target="tpu_custom_call" | custom-call | tf_op jit(solution)/shard_map/pallas_call | solution.py:451
  15.2 0.0 collective-permute-done.refs_1_.refs_3_
  15.3 4.1 %shard_map.61 = (f32[1024,2048]{1,0:T(8,128)S(1)}, f32[1024,2048]{1,0:T(8,128)S(1)}) custom-call(bf16[64,4224]{1,0:T(8,128)(2,1)S(1)} %get-tuple-element.27.refs_0_.refs_2_, bf16[64,4224]{1,0:T(8,128)(2,1)S(1)} %collective-permute-done.refs_1_.refs_3_, bf16[128,128]{1,0:T(8,128)(2,1)S(1)} %get-tuple-element.28.refs_2_), custom_call_target="tpu_custom_call" | custom-call | tf_op jit(solution)/shard_map/pallas_call | solution.py:451
  19.3 0.0 collective-permute-done.3.refs_5_
  19.4 2.7 %shard_map.62 = (f32[1024,2048]{1,0:T(8,128)S(1)}, f32[16,128]{1,0:T(8,128)S(1)}, f32[1024,128]{1,0:T(8,128)S(1)}, f32[16,128]{1,0:T(8,128)S(1)}, f32[1024,128]{...) custom-call(f32[32,128]{1,0:T(8,128)S(1)} %get-tuple-element.26.refs_0_.refs_2_, ...), custom_call_target="tpu_custom_call" | custom-call | tf_op jit(solution)/shard_map/pallas_call | solution.py:451
  22.0 0.0 collective-permute-done.1.refs_4_
  22.1 0.3 collective-permute-start.4
  22.3 1.3 %collective-permute-done.4.refs_5_ = bf16[64,2048]{1,0:T(8,128)(2,1)S(1)} collective-permute-done((bf16[64,2048]{1,0:T(8,128)(2,1)S(1)}, bf16[64,2048]{1,0:T(8,128)(2,1)S(1)}, u32[]{:S(2)}, u32[]{:S(2)}) %collective-permute-start.4) | collective-permute-done | bytes 262176 | tf_op jit(solution)/shard_map/ppermute | solution.py:528
  23.7 2.2 %shard_map.63 = (f32[1024,2048]{1,0:T(8,128)S(1)}, f32[16,128]{1,0:T(8,128)S(1)}, f32[32,8,128]{2,1,0:T(8,128)S(1)}) custom-call(f32[32,128]{1,0:T(8,128)S(1)} %get-tuple-element.26.refs_0_.refs_2_, f32[1024,2048]{1,0:T(8,128)S(1)} %get-tuple-element.29.refs_1_, bf16[64,4224]{1,0:T(8,128)(2,1)S(1)} %get-tuple-element.27.refs_0_.refs_2_, ...), custom_call_target="tpu_custom_call" | custom-call | tf_op jit(solution)/shard_map/pallas_call | solution.py:451
  25.9 12.5 %all_to_all.10.refs_0_ = f32[32,8,128]{2,1,0:T(8,128)S(1)} all-to-all(f32[32,8,128]{2,1,0:T(8,128)S(1)} %get-tuple-element.44), channel_id=1, replica_groups=mesh['frames'=4,'win'=8] {'frames','win'}, dimensions={0} | all-to-all | bytes 262144 | tf_op jit(solution)/shard_map/all_to_all | solution.py:445
  38.4 0.1 shard_map.64.refs_0_
  38.5 0.2 collective-permute-start.5
  38.6 1.1 %collective-permute-done.5.refs_1_ = f32[3,16,128]{2,1,0:T(8,128)S(1)} collective-permute-done((f32[3,16,128]{2,1,0:T(8,128)S(1)}, f32[3,16,128]{2,1,0:T(8,128)S(1)}, u32[]{:S(2)}, u32[]{:S(2)}) %collective-permute-start.5) | collective-permute-done | bytes 24608 | tf_op jit(solution)/shard_map/ppermute | solution.py:557
  39.7 3.2 %shard_map.65 = (f32[32,8,128]{2,1,0:T(8,128)S(1)}, f32[8,128]{1,0:T(8,128)S(1)}, f32[32,128]{1,0:T(8,128)S(1)}) custom-call(f32[3,16,128]{2,1,0:T(8,128)S(1)} %shard_map.64.refs_0_, f32[3,16,128]{2,1,0:T(8,128)S(1)} %collective-permute-done.5.refs_1_, f32[32,128]{1,0:T(8,128)S(1)} %get-tuple-element.26.refs_0_.refs_2_, ...), custom_call_target="tpu_custom_call" | custom-call | tf_op jit(solution)/shard_map/pallas_call | solution.py:451
  42.9 10.0 %all_to_all.11.given = f32[32,8,128]{2,1,0:T(8,128)S(1)} all-to-all(f32[32,8,128]{2,1,0:T(8,128)S(1)} %get-tuple-element.47), channel_id=1, replica_groups=mesh['frames'=4,'win'=8] {'frames','win'}, dimensions={0} | all-to-all | bytes 262144 | tf_op jit(solution)/shard_map/all_to_all | solution.py:445
  52.9 0.8 %shard_map.66 = (f32[1024]{0:T(1024)}, f32[1,1024]{1,0:T(1,128)}) custom-call(f32[32,8,128]{2,1,0:T(8,128)S(1)} %all_to_all.11.given, f32[32,128]{1,0:T(8,128)S(1)} %get-tuple-element.48.state_counts, f32[8,128]{1,0:T(8,128)S(1)} %get-tuple-element.49.logs), custom_call_target="tpu_custom_call" | custom-call | tf_op jit(solution)/shard_map/pallas_call | solution.py:451
Async XLA Ops:
  2.1 9.7 %collective-permute-start.2 = (bf16[64,2176]{1,0:T(8,128)(2,1)S(1)}, bf16[64,2176]{1,0:T(8,128)(2,1)S(1)}, u32[]{:S(2)}, u32[]{:S(2)}) collective-permute-start(bf16[64,2176]{1,0:T(8,128)(2,1)S(1)} %get-tuple-element.32), channel_id=1, source_target_pairs={{16,0},{24,8},{0,16},{8,24},{17,1},{25,9},{1,17},{9,25},{18,2},{26... | collective-permute-start | bytes 835592 | tf_op jit(solution)/shard_map/ppermute | solution.py:493
  5.1 10.1 %collective-permute-start = (bf16[64,4224]{1,0:T(8,128)(2,1)S(1)}, bf16[64,4224]{1,0:T(8,128)(2,1)S(1)}, u32[]{:S(2)}, u32[]{:S(2)}) collective-permute-start(bf16[64,4224]{1,0:T(8,128)(2,1)S(1)} %get-tuple-element.27.refs_0_.refs_2_), channel_id=1, source_target_pairs={{0,8},{8,0},{16,24},{24,16},{1,9},{9,1},{17,25},{25,17},{2,10},{10... | collective-permute-start | bytes 1622024 | tf_op jit(solution)/shard_map/ppermute | solution.py:494
  11.8 7.6 %collective-permute-start.3 = (bf16[64,2176]{1,0:T(8,128)(2,1)S(1)}, bf16[64,2176]{1,0:T(8,128)(2,1)S(1)}, u32[]{:S(2)}, u32[]{:S(2)}) collective-permute-start(bf16[64,2176]{1,0:T(8,128)(2,1)S(1)} %collective-permute-done.2.refs_4_), channel_id=1, source_target_pairs={{0,8},{8,0},{16,24},{24,16},{1,9},{9,1},{17,25},{25,17},{2,10},{10... | collective-permute-start | bytes 835592 | tf_op jit(solution)/shard_map/ppermute | solution.py:528
  11.8 10.3 %collective-permute-start.1 = (bf16[64,2048]{1,0:T(8,128)(2,1)S(1)}, bf16[64,2048]{1,0:T(8,128)(2,1)S(1)}, u32[]{:S(2)}, u32[]{:S(2)}) collective-permute-start(bf16[64,2048]{1,0:T(8,128)(2,1)S(1)} %get-tuple-element.30), channel_id=1, source_target_pairs={{16,0},{24,8},{0,16},{8,24},{17,1},{25,9},{1,17},{9,25},{18,2},{26... | collective-permute-start | bytes 786440 | tf_op jit(solution)/shard_map/ppermute | solution.py:493
  22.1 1.6 %collective-permute-start.4 = (bf16[64,2048]{1,0:T(8,128)(2,1)S(1)}, bf16[64,2048]{1,0:T(8,128)(2,1)S(1)}, u32[]{:S(2)}, u32[]{:S(2)}) collective-permute-start(bf16[64,2048]{1,0:T(8,128)(2,1)S(1)} %collective-permute-done.1.refs_4_), channel_id=1, source_target_pairs={{0,8},{8,0},{16,24},{24,16},{1,9},{9,1},{17,25},{25,17},{2,10},{10... | collective-permute-start | bytes 786440 | tf_op jit(solution)/shard_map/ppermute | solution.py:528
  38.5 1.3 %collective-permute-start.5 = (f32[3,16,128]{2,1,0:T(8,128)S(1)}, f32[3,16,128]{2,1,0:T(8,128)S(1)}, u32[]{:S(2)}, u32[]{:S(2)}) collective-permute-start(f32[3,16,128]{2,1,0:T(8,128)S(1)} %shard_map.64.refs_0_), channel_id=1, source_target_pairs={{0,8},{8,0},{16,24},{24,16},{1,9},{9,1},{17,25},{25,17},{2,10},{10... | collective-permute-start | bytes 73736 | tf_op jit(solution)/shard_map/ppermute | solution.py:557
